TPU v7x, 32 devices: a whole 2x2x4 slice. The times are simulated.
32 devices in a mesh: groups: 2 (over x), dom: 16 (over z, y, core).
Axes of the slice: x: 2, y: 2, z: 4, core: 2. Of those that a mesh axis runs over, the one named last changes fastest.
Arguments:
- grid: bfloat16 [32768, 1024], P(('groups', 'dom')), parts along dimension 0, may hold values from -6 to 6
- latent_in: bfloat16 [512, 1024], P(('groups', 'dom')), parts along dimension 0, may hold values from -3 to 3
- grid_gain: float32 [1024], replicated, may hold values from 0.5 to 1.5
- node_gain: float32 [1024], replicated, may hold values from 0.5 to 1.5
- dec_gain: float32 [1024], replicated, may hold values from 0.5 to 1.5
- w_q_enc: bfloat16 [1024, 512], replicated
- w_kv_enc: bfloat16 [1024, 1024], replicated, may hold values from -0.1875 to 0.1875
- w_o_enc: bfloat16 [512, 1024], replicated, may hold values from -0.25 to 0.25
- w_q_dec: bfloat16 [1024, 512], replicated
- w_kv_dec: bfloat16 [1024, 1024], replicated, may hold values from -0.1875 to 0.1875
- w_o_dec: bfloat16 [512, 1024], replicated, may hold values from -0.25 to 0.25
- enc_need: int32 [16, 512], P('dom'), may hold values from 0 to 1023
- enc_slot: int32 [32, 256], P(None, 'dom'), may hold values from 0 to 511
- enc_count: int32 [256], P('dom'), may hold values from 1 to 32
- dec_need: int32 [16, 4096], P('dom'), may hold values from 0 to 15
- dec_slot: int32 [4, 16384], P(None, 'dom'), may hold values from 0 to 4095
Outputs:
- latent_out: bfloat16 [512, 1024], P(('groups', 'dom')), parts along dimension 0
- grid_out: bfloat16 [32768, 1024], P(('groups', 'dom')), parts along dimension 0
There are 2 independent parts, one for each index of `groups`. A program takes and returns all parts, laid end to end along the dimension named above; an argument that names none is the same for every part. Nothing has to cross between parts.
Inputs may be any that keep to these rules, and one draw needn't show every extreme that they name: `enc_need`: a grid point's index within its band; entries may repeat. Edges of node n are enc_slot[0..enc_count[n]-1, n]; entries may repeat. `dec_need`: a latent node's index within its window; entries may repeat. `dec_slot`: entries may repeat.
All inputs are finite; a program needn't handle non-finite values.
Results may differ from a plain program's by a relative error of at most 0.02.
The roundings to bfloat16 on the way count: a program that leaves them out, or rounds other values in their place, can miss the bound.
Values may be sent and summed in bfloat16 or wider, within the bound.
A program may use at most 128 MiB of HBM per device.

v0:
```python
import functools
import math

import jax
import jax.numpy as jnp
from jax import lax
from jax.experimental import pallas as pl
from jax.experimental.pallas import tpu as pltpu
from jax.sharding import PartitionSpec as P

HEADS = 8
norm_eps = 1e-06
F32 = jnp.float32
BF16 = jnp.bfloat16


def rms_norm(values, weight_gain):
    widened = values.astype(F32)
    spread = jnp.mean(widened * widened, axis=-1, keepdims=True)
    return (widened * lax.rsqrt(spread + norm_eps) * weight_gain).astype(BF16)


def attend_dense(queries, pairs, edges):
    rows, width = queries.shape
    head = width // HEADS
    q = queries.reshape(rows, HEADS, head)
    k = pairs[:, :width].reshape(-1, HEADS, head)
    v = pairs[:, width:].reshape(-1, HEADS, head)
    scores = jnp.einsum("rhd,khd->hrk", q, k, preferred_element_type=F32)
    scores = jnp.where(edges[None] > 0, scores * (1.0 / math.sqrt(head)), -1e30)
    highest = jnp.max(scores, axis=-1, keepdims=True)
    raised = jnp.exp(scores - highest) * edges[None]
    weights = (raised / jnp.sum(raised, axis=-1, keepdims=True)).astype(BF16)
    mixed = jnp.einsum("hrk,khd->rhd", weights, v, preferred_element_type=F32)
    return mixed.reshape(rows, width).astype(BF16)


def on_device(grid, latent_in, grid_gain, node_gain, dec_gain, w_q_enc, w_kv_enc, w_o_enc,
              w_q_dec, w_kv_dec, w_o_dec, enc_need, enc_slot, enc_count, dec_need, dec_slot):
    peers = lax.axis_size("dom")
    nodes = latent_in.shape[0]
    normed_grid = rms_norm(grid, grid_gain)
    wanted = lax.all_to_all(enc_need.reshape(peers, -1), "dom", split_axis=0, concat_axis=0, tiled=True)
    band = jnp.arange(grid.shape[0], dtype=jnp.int32)
    pick = (wanted.reshape(-1)[:, None] == band[None, :]).astype(BF16)
    chosen = jnp.dot(pick, normed_grid, preferred_element_type=F32).astype(BF16)
    rows = jnp.dot(chosen, w_kv_enc, preferred_element_type=F32).astype(BF16)
    arrived = lax.all_to_all(rows, "dom", split_axis=0, concat_axis=0, tiled=True)
    enc_queries = jnp.dot(rms_norm(latent_in, node_gain), w_q_enc, preferred_element_type=F32).astype(BF16)
    live = jnp.arange(enc_slot.shape[0], dtype=jnp.int32)[:, None] < enc_count[None, :]
    slot_row = jnp.arange(enc_need.shape[1], dtype=jnp.int32)
    enc_edges = jnp.sum((live[:, :, None] & (enc_slot[:, :, None] == slot_row)).astype(F32), axis=0)
    enc_mixed = attend_dense(enc_queries, arrived, enc_edges)
    enc_update = jnp.dot(enc_mixed, w_o_enc, preferred_element_type=F32)
    latent_out = (latent_in.astype(F32) + enc_update).astype(BF16)
    latent_pairs = jnp.dot(rms_norm(latent_out, dec_gain), w_kv_dec, preferred_element_type=F32).astype(BF16)
    dec_queries = jnp.dot(normed_grid, w_q_dec, preferred_element_type=F32).astype(BF16)
    everyone = lax.all_gather(latent_pairs, "dom", axis=0, tiled=True)
    total = dec_need.shape[1]
    cap = total // peers
    lanes = 128
    table = dec_need.reshape(total // lanes, lanes).astype(BF16)
    high = (dec_slot // lanes)[:, :, None] == jnp.arange(total // lanes, dtype=jnp.int32)
    low = (dec_slot % lanes)[:, :, None] == jnp.arange(lanes, dtype=jnp.int32)
    need = jnp.einsum("jgt,tl->jgl", high.astype(BF16), table, preferred_element_type=F32)
    need = jnp.sum(jnp.where(low, need, 0.0), axis=-1).astype(jnp.int32)
    node = (dec_slot // cap) * nodes + need
    dec_edges = jnp.sum((node[:, :, None] == jnp.arange(peers * nodes, dtype=jnp.int32)).astype(F32), axis=0)
    dec_mixed = attend_dense(dec_queries, everyone, dec_edges)
    dec_update = jnp.dot(dec_mixed, w_o_dec, preferred_element_type=F32)
    grid_out = (grid.astype(F32) + dec_update).astype(BF16)
    return (latent_out, grid_out)


NT = (((1,), (1,)), ((), ()))
TN = (((0,), (0,)), ((), ()))
HIGH = lax.Precision.HIGHEST


def iota(shape, dim):
    return lax.broadcasted_iota(jnp.int32, shape, dim)


def norm_into(values, gain):
    widened = values.astype(F32)
    spread = jnp.mean(widened * widened, axis=-1, keepdims=True)
    return (widened * lax.rsqrt(spread + norm_eps) * gain).astype(BF16)


def encoder_kernel(
    peers, grid_hbm, latent_ref, ggain_ref, ngain_ref, dgain_ref, wq_hbm, wkv_hbm, wo_hbm, wqd_hbm, wkvd_hbm,
    need_ref, slot_ref, count_ref, dslot_ref, table_ref,
    latent_out, pairs_out, queries_hbm, bias_hbm,
    grid_v, wq_v, wkv_v, wo_v, wqd_v, wkvd_v, normed, rows, query_mine, edges_mine,
    need_all, query_all, edges_all, times_all, mix_send, stat_send, mix_all, stat_all, pairs_all,
    queries_out, bias_out, load_sem, store_sem, send_sem, recv_sem,
):
    me = lax.axis_index("dom")
    nodes, model = latent_ref.shape
    width = wq_v.shape[1]
    head = width // HEADS
    cap = need_ref.shape[1] // peers
    group = 128 // cap
    chips = peers // 2
    side = lax.rem(me, 2)
    partner = me + 1 - 2 * side
    points = grid_v.shape[0]
    lanes = HEADS * nodes

    loads = [
        pltpu.make_async_copy(source, target, load_sem.at[number])
        for number, (source, target) in enumerate(
            ((wq_hbm, wq_v), (grid_hbm, grid_v), (wkv_hbm, wkv_v), (wqd_hbm, wqd_v), (wo_hbm, wo_v), (wkvd_hbm, wkvd_v))
        )
    ]
    for load in loads:
        load.start()

    barrier = pltpu.get_barrier_semaphore()
    for step in range(1, peers):
        pl.semaphore_signal(
            barrier, inc=1, device_id={"dom": lax.rem(me + step, peers)}, device_id_type=pl.DeviceIdType.MESH
        )

    def message(kind, source, target, to, slot, way=None):
        return pltpu.make_async_remote_copy(
            src_ref=source,
            dst_ref=target,
            send_sem=send_sem.at[kind, to if way is None else way],
            recv_sem=recv_sem.at[kind, slot],
            device_id={"dom": to},
            device_id_type=pl.DeviceIdType.MESH,
        )

    def need_to(to, slot):
        return message(0, need_ref, need_all.at[slot], to, slot)

    def query_to(to, slot):
        return message(1, query_mine, query_all.at[slot], to, slot)

    def query_on(owner, slot):
        return message(6, query_all.at[owner], query_all.at[slot], partner, slot, owner)

    def pairs_on(owner, slot):
        return message(7, pairs_all.at[owner], pairs_all.at[slot], partner, slot, owner)

    def edges_to(to, slot):
        return message(2, edges_mine.at[to // group], edges_all.at[slot], to, slot)

    def mix_to(to, slot):
        return message(3, mix_send.at[to], mix_all.at[slot], to, slot)

    def stat_to(to, slot):
        return message(4, stat_send.at[to], stat_all.at[slot], to, slot)

    def pairs_to(to, slot):
        return message(5, pairs_all.at[me], pairs_all.at[slot], to, slot)

    def each_peer(act):
        def body(step, carry):
            act(lax.rem(me + step, peers))
            return carry

        lax.fori_loop(1, peers, body, 0)

    def each_chip(act):
        def body(step, carry):
            act(lax.rem(me + 2 * step, peers))
            return carry

        lax.fori_loop(1, chips, body, 0)

    edge_total = slot_ref.shape[1]
    own = iota((nodes, nodes), 0) == iota((nodes, nodes), 1)
    counts = jnp.sum(jnp.where(own, count_ref[...].astype(F32), 0.0), axis=1, keepdims=True)
    slots = jnp.where(iota(slot_ref.shape, 1).astype(F32) < counts, slot_ref[...], -1)
    entry = iota((nodes, peers * cap), 1)
    tally = jnp.zeros((nodes, peers * cap), F32)
    for j in range(edge_total):
        tally = tally + jnp.where(slots[:, j : j + 1] == entry, 1.0, 0.0)
    tally = tally.astype(BF16)
    for part in range(peers // group):
        edges_mine[part] = tally[:, part * 128 : (part + 1) * 128]
    edges_all[me] = edges_mine[me // group]
    loads[0].wait()
    queries = jnp.dot(
        norm_into(latent_ref[...], ngain_ref[...]), wq_v[...], preferred_element_type=F32
    ).astype(BF16)
    query_mine[...] = queries
    query_all[me] = queries
    need_all[me] = need_ref[...]

    pl.semaphore_wait(barrier, peers - 1)
    each_peer(lambda to: need_to(to, me).start())
    query_to(partner, me).start()
    each_chip(lambda to: query_to(to, me).start())
    each_peer(lambda to: edges_to(to, me).start())

    loads[1].wait()

    def norm_block(block, carry):
        at = pl.ds(pl.multiple_of(block * 128, 128), 128)
        normed[at, :] = norm_into(grid_v[at, :], ggain_ref[...])
        return carry

    lax.fori_loop(0, points // 128, norm_block, 0)

    each_peer(lambda peer: need_to(peer, peer).wait_recv())
    lists = need_all[...]
    asked = jnp.broadcast_to(lists, (peers, cap, peers * cap))
    mine = iota((peers, cap, peers * cap), 2) == me * cap + iota((peers, cap, peers * cap), 1)
    wanted = jnp.sum(jnp.where(mine, asked.astype(F32), 0.0), axis=2, keepdims=True).astype(jnp.int32)
    wanted = wanted.reshape(peers * cap, 1)
    pick = jnp.where(wanted == iota((peers * cap, points), 1), 1.0, 0.0).astype(BF16)
    chosen = jnp.dot(pick, normed[...], preferred_element_type=F32).astype(BF16)
    def pass_query(peer):
        query_to(peer, peer).wait_recv()
        query_on(peer, peer).start()


    loads[2].wait()
    rows[...] = jnp.dot(chosen, wkv_v[...], preferred_element_type=F32).astype(BF16)

    each_chip(pass_query)
    each_peer(lambda peer: edges_to(peer, peer).wait_recv())
    mine = iota((cap, 128), 1) == lax.rem(me, group) * cap + iota((cap, 128), 0)
    entries = lax.dot_general(
        mine.astype(BF16), edges_all[...].reshape(peers * nodes, 128), NT, preferred_element_type=F32
    ).astype(BF16)
    fan = iota((peers * nodes, peers * lanes), 0)
    fan_lane = iota((peers * nodes, peers * lanes), 1)
    fan = fan == (fan_lane // lanes) * nodes + lax.rem(fan_lane, nodes)
    entries = jnp.dot(entries, jnp.where(fan, 1.0, 0.0).astype(BF16), preferred_element_type=F32)
    for peer in range(peers):
        times_all[peer] = entries[:, peer * lanes : (peer + 1) * lanes]

    own_head = iota((lanes, width), 0) // nodes == iota((lanes, width), 1) // head

    def window(w):
        spread_query = jnp.broadcast_to(query_all[w][None], (HEADS, nodes, width)).reshape(lanes, width)
        spread_query = jnp.where(own_head, spread_query, jnp.zeros_like(spread_query))
        here = pl.ds(pl.multiple_of(w * cap, cap), cap)
        scores = lax.dot_general(rows[here, :width], spread_query, NT, preferred_element_type=F32)
        times = times_all[w]
        scores = jnp.where(times > 0, scores * (1.0 / math.sqrt(head)), -1e30)
        highest = jnp.max(scores, axis=0, keepdims=True)
        raised = jnp.exp(scores - highest) * times
        total = jnp.sum(raised, axis=0, keepdims=True)
        mixed = lax.dot_general(raised.astype(BF16), rows[here, width:], TN, preferred_element_type=F32)
        mixed = jnp.where(own_head, mixed, 0.0).reshape(HEADS, nodes, width)
        return jnp.sum(mixed, axis=0).astype(BF16), highest, total

    def serve(windows):
        for peer, answer in [(peer, window(peer)) for peer in windows]:
            mix_send[peer] = answer[0]
            stat_send[peer, 0:1, :] = answer[1]
            stat_send[peer, 1:2, :] = answer[2]

    def reply(peer):
        mix_to(peer, me).start()
        stat_to(peer, me).start()

    serve([lax.rem(me + 2 * step, peers) for step in range(1, chips)])
    each_chip(reply)
    query_to(partner, partner).wait_recv()

    def take_passed(peer):
        owner = peer + 1 - 2 * side
        query_on(owner, owner).wait_recv()

    each_chip(take_passed)
    serve([lax.rem(partner + 2 * step, peers) for step in range(chips)])
    lax.fori_loop(0, chips, lambda step, carry: (reply(lax.rem(partner + 2 * step, peers)), carry)[1], 0)
    mixed, highest, total = window(me)
    mix_all[me] = mixed
    stat_all[me, 0:1, :] = highest
    stat_all[me, 1:2, :] = total

    loads[3].wait()
    queries_out[...] = jnp.dot(normed[...], wqd_v[...], preferred_element_type=F32).astype(BF16)
    queries_store = pltpu.make_async_copy(queries_out, queries_hbm, store_sem.at[0])
    queries_store.start()

    keys = peers * nodes
    dec_cap = table_ref.shape[0] * 128 // peers
    slots = dslot_ref[...]
    edge_total = slots.shape[0]
    slots = jnp.concatenate([slots] * (8 // edge_total), axis=0)
    columns = []
    for part in range(points // 128):
        piece = slots[:, part * 128 : (part + 1) * 128]
        high = piece // 128
        low = lax.rem(piece, 128)
        need = jnp.zeros_like(piece)
        for line in range(table_ref.shape[0]):
            entry = jnp.broadcast_to(table_ref[line : line + 1, :], piece.shape)
            need = jnp.where(high == line, jnp.take_along_axis(entry, low, axis=1), need)
        columns.append((piece // dec_cap) * nodes + need)
    node = jnp.concatenate(columns, axis=1)
    name = iota((keys, points), 0)
    times = jnp.zeros((keys, points), F32)
    for j in range(edge_total):
        times = times + jnp.where(node[j : j + 1, :] == name, 1.0, 0.0)
    bias_out[...] = jnp.where(times > 0, jnp.log(jnp.maximum(times, 1.0)), -1e30)
    bias_store = pltpu.make_async_copy(bias_out, bias_hbm, store_sem.at[1])
    bias_store.start()

    def take_mix(peer):
        mix_to(peer, peer).wait_recv()
        stat_to(peer, peer).wait_recv()

    each_peer(take_mix)
    tops = [stat_all[peer, 0:1, :] for peer in range(peers)]
    sums = [stat_all[peer, 1:2, :] for peer in range(peers)]
    top = functools.reduce(jnp.maximum, tops)
    shares = [jnp.exp(one - top) for one in tops]
    whole = functools.reduce(jnp.add, [a * b for a, b in zip(shares, sums)])
    own_node = iota((nodes, lanes), 0) == lax.rem(iota((nodes, lanes), 1), nodes)
    stacked = jnp.concatenate([jnp.where(own_node, share / whole, 0.0) for share in shares], axis=0)
    widen = (iota((lanes, width), 0) // nodes == iota((lanes, width), 1) // head).astype(F32)
    factors = jnp.dot(stacked, widen, precision=HIGH, preferred_element_type=F32).reshape(peers, nodes, width)
    enc_mixed = jnp.sum(factors * mix_all[...].astype(F32), axis=0).astype(BF16)
    loads[4].wait()
    update = jnp.dot(enc_mixed, wo_v[...], preferred_element_type=F32)
    fresh = (latent_ref[...].astype(F32) + update).astype(BF16)
    latent_out[...] = fresh
    loads[5].wait()
    pairs = jnp.dot(norm_into(fresh, dgain_ref[...]), wkvd_v[...], preferred_element_type=F32).astype(BF16)
    pairs_all[me] = pairs
    each_chip(lambda to: pairs_to(to, me).start())
    pairs_to(partner, me).start()

    def pass_pairs(peer):
        pairs_to(peer, peer).wait_recv()
        pairs_on(peer, peer).start()

    each_chip(pass_pairs)
    pairs_to(partner, partner).wait_recv()

    def take_pairs(peer):
        owner = peer + 1 - 2 * side
        pairs_on(owner, owner).wait_recv()

    each_chip(take_pairs)
    pairs_out[...] = pairs_all[...].reshape(peers * nodes, model)

    def drain(to):
        for outgoing in (need_to, edges_to, mix_to, stat_to):
            outgoing(to, me).wait_send()

    def drain_chip(to):
        query_to(to, me).wait_send()
        pairs_to(to, me).wait_send()
        query_on(to, to).wait_send()
        pairs_on(to, to).wait_send()

    queries_store.wait()
    bias_store.wait()
    each_peer(drain)
    each_chip(drain_chip)
    query_to(partner, me).wait_send()
    pairs_to(partner, me).wait_send()


def encode(grid, latent_in, grid_gain, node_gain, dec_gain, w_q_enc, w_kv_enc, w_o_enc, w_q_dec, w_kv_dec,
           enc_need, enc_slot, enc_count, dec_slot, dec_need):
    peers = lax.axis_size("dom")
    nodes, model = latent_in.shape
    width = w_q_enc.shape[1]
    entries = enc_need.shape[1]
    cap = entries // peers
    points = grid.shape[0]
    vmem = pl.BlockSpec(memory_space=pltpu.VMEM)
    far = pl.BlockSpec(memory_space=pl.ANY)
    return pl.pallas_call(
        functools.partial(encoder_kernel, peers),
        name="encode",
        out_shape=(
            jax.ShapeDtypeStruct((nodes, model), BF16),
            jax.ShapeDtypeStruct((peers * nodes, 2 * width), BF16),
            jax.ShapeDtypeStruct((points, width), BF16),
            jax.ShapeDtypeStruct((peers * nodes, points), F32),
        ),
        in_specs=[far, vmem, vmem, vmem, vmem, far, far, far, far, far, vmem, vmem, vmem, vmem, vmem],
        out_specs=(vmem, vmem, far, far),
        scratch_shapes=[
            pltpu.VMEM(grid.shape, BF16),
            pltpu.VMEM(w_q_enc.shape, BF16),
            pltpu.VMEM(w_kv_enc.shape, BF16),
            pltpu.VMEM(w_o_enc.shape, BF16),
            pltpu.VMEM(w_q_dec.shape, BF16),
            pltpu.VMEM(w_kv_dec.shape, BF16),
            pltpu.VMEM(grid.shape, BF16),
            pltpu.VMEM((entries, 2 * width), BF16),
            pltpu.VMEM((nodes, width), BF16),
            pltpu.VMEM((entries // 128, nodes, 128), BF16),
            pltpu.VMEM((peers, 1, entries), jnp.int32),
            pltpu.VMEM((peers, nodes, width), BF16),
            pltpu.VMEM((peers, nodes, 128), BF16),
            pltpu.VMEM((peers, cap, HEADS * nodes), F32),
            pltpu.VMEM((peers, nodes, width), BF16),
            pltpu.VMEM((peers, 2, HEADS * nodes), F32),
            pltpu.VMEM((peers, nodes, width), BF16),
            pltpu.VMEM((peers, 2, HEADS * nodes), F32),
            pltpu.VMEM((peers, nodes, 2 * width), BF16),
            pltpu.VMEM((points, width), BF16),
            pltpu.VMEM((peers * nodes, points), F32),
            pltpu.SemaphoreType.DMA((6,)),
            pltpu.SemaphoreType.DMA((2,)),
            pltpu.SemaphoreType.DMA((8, peers)),
            pltpu.SemaphoreType.DMA((8, peers)),
        ],
        compiler_params=pltpu.CompilerParams(
            collective_id=0, has_side_effects=True, vmem_limit_bytes=60 * 1024 * 1024
        ),
    )(grid, latent_in, grid_gain[None], node_gain[None], dec_gain[None], w_q_enc, w_kv_enc, w_o_enc, w_q_dec,
      w_kv_dec, enc_need, enc_slot.T, enc_count[None], dec_slot, dec_need.reshape(-1, 128))


def decoder_kernel(query_ref, pairs_ref, bias_ref, grid_hbm, wo_hbm, latent_ref, out_hbm, latent_out, keys_of, turned, mixed,
                   grid_v, wo_v, out_v, load_sem, store_sem):
    tile, width = query_ref.shape
    head = width // HEADS
    keys = pairs_ref.shape[0]
    quad = 4
    load_wo = pltpu.make_async_copy(wo_hbm, wo_v, load_sem.at[0])
    load_grid = pltpu.make_async_copy(grid_hbm, grid_v, load_sem.at[1])
    load_wo.start()
    load_grid.start()

    turned[...] = pairs_ref[:, width:].astype(F32).T.astype(BF16)
    latent_out[...] = latent_ref[...]
    lane_head = iota((keys, quad * head), 1) // head
    for h in range(HEADS):
        some = pairs_ref[:, (h // quad) * quad * head : (h // quad + 1) * quad * head] * (1.0 / math.sqrt(head))
        keys_of[h // quad, (h % quad) * keys : (h % quad + 1) * keys, :] = jnp.where(
            lane_head == h % quad, some, jnp.zeros_like(some)
        )

    for four in range(HEADS // quad):
        query = query_ref[:, four * quad * head : (four + 1) * quad * head]
        for side in range(quad):
            h = four * quad + side
            own = keys_of[four, side * keys : (side + 1) * keys, :]
            scores = lax.dot_general(own, query, NT, preferred_element_type=F32) + bias_ref[...]
            highest = jnp.max(scores, axis=0, keepdims=True)
            raised = jnp.exp(scores - highest)
            total = jnp.sum(raised, axis=0, keepdims=True)
            got = jnp.dot(turned[h * head : (h + 1) * head, :], raised.astype(BF16), preferred_element_type=F32)
            mixed[h * head : (h + 1) * head, :] = (got / total).astype(BF16)
    load_wo.wait()
    load_grid.wait()
    stores = []
    block = tile // 4
    for part in range(4):
        at = slice(part * block, (part + 1) * block)
        update = lax.dot_general(mixed[:, at], wo_v[...], TN, preferred_element_type=F32)
        out_v[at, :] = (grid_v[at, :].astype(F32) + update).astype(BF16)
        stores.append(pltpu.make_async_copy(out_v.at[at], out_hbm.at[at], store_sem.at[part]))
        stores[-1].start()
    for store in stores:
        store.wait()


def decode(queries, pairs, bias, grid, w_o_dec, latent_out):
    points, model = grid.shape
    width = queries.shape[1]
    tile = points
    vmem = pl.BlockSpec(memory_space=pltpu.VMEM)
    far = pl.BlockSpec(memory_space=pl.ANY)
    return pl.pallas_call(
        decoder_kernel,
        name="decode",
        out_shape=(
            jax.ShapeDtypeStruct(grid.shape, BF16),
            jax.ShapeDtypeStruct(latent_out.shape, BF16),
        ),
        in_specs=[vmem, vmem, vmem, far, far, vmem],
        out_specs=(far, vmem),
        scratch_shapes=[pltpu.VMEM((2, 4 * pairs.shape[0], width // 2), BF16), pltpu.VMEM((width, pairs.shape[0]), BF16), pltpu.VMEM((width, tile), BF16),
                        pltpu.VMEM(grid.shape, BF16), pltpu.VMEM(w_o_dec.shape, BF16), pltpu.VMEM(grid.shape, BF16),
                        pltpu.SemaphoreType.DMA((2,)), pltpu.SemaphoreType.DMA((4,))],
    )(queries, pairs, bias, grid, w_o_dec, latent_out)


def by_kernels(grid, latent_in, grid_gain, node_gain, dec_gain, w_q_enc, w_kv_enc, w_o_enc,
               w_q_dec, w_kv_dec, w_o_dec, enc_need, enc_slot, enc_count, dec_need, dec_slot):
    latent_out, pairs, queries, bias = encode(
        grid, latent_in, grid_gain, node_gain, dec_gain, w_q_enc, w_kv_enc, w_o_enc, w_q_dec, w_kv_dec,
        enc_need, enc_slot, enc_count, dec_slot, dec_need)
    grid_out, latent_out = decode(queries, pairs, bias, grid, w_o_dec, latent_out)
    return (latent_out, grid_out)


def chosen_form(*args):
    grid, latent_in, enc_need, dec_slot = args[0], args[1], args[11], args[15]
    peers = lax.axis_size("dom")
    cap = enc_need.shape[1] // peers
    small = latent_in.shape[0] * peers <= 256
    fits = peers % 2 == 0 and 128 % cap == 0 and cap % 32 == 0 and HEADS * latent_in.shape[0] == 128 and grid.shape[0] % 512 == 0
    if small and fits and 8 % dec_slot.shape[0] == 0:
        return by_kernels(*args)
    return on_device(*args)


def solution(mesh):
    both, rep = P(("groups", "dom"), None), P()
    return jax.shard_map(
        chosen_form,
        mesh=mesh,
        in_specs=(both, both, *([rep] * 9), P("dom", None), P(None, "dom"), P("dom"), P("dom", None), P(None, "dom")),
        out_specs=(both, both),
        check_vma=False,
    )
```

profile of v0, /device:TPU:1, one launch (start us, length us, event | category | flops | bytes accessed | tf_op | source)
XLA Modules:
  0.0 43.6 jit_solution(18145427265022984165)
XLA Ops:
  0.6 34.1 %encode.1 = (bf16[16,1024]{1,0:T(8,128)(2,1)}, bf16[256,1024]{1,0:T(8,128)(2,1)}, bf16[1024,512]{1,0:T(8,128)(2,1)}, f32[256,1024]{1,0:T(8,128)}) custom-call(bf16[1024,1024]{1,0:T(8,128)(2,1)} %grid_hbm.3, bf16[16,1024]{1,0:T(8,128)(2,1)} %latent_ref.1, f32[1,1024]{1,0:T(1,128)} %bitcast.8, f32[1,1024]{1,0:T(1,128)} %bitcast.9, f32[1,1024]{1,0:T(1,128)} %bitcast.10, ...), custom_call_target="tpu_custom_call" | custom-call | tf_op jit(solution)/shard_map/encode/pallas_call | solution.py:375
  34.8 8.9 %decode.1 = (bf16[1024,1024]{1,0:T(8,128)(2,1)}, bf16[16,1024]{1,0:T(8,128)(2,1)}) custom-call(bf16[1024,512]{1,0:T(8,128)(2,1)} %get-tuple-element.8.query_ref, bf16[256,1024]{1,0:T(8,128)(2,1)} %get-tuple-element.9.pairs_ref, f32[256,1024]{1,0:T(8,128)} %get-tuple-element.10.bias_ref, bf16[1024,1024]{1,0:T(8,128)(2,1)} %grid_hbm.3, ...), custom_call_target="tpu_custom_call" | custom-call | tf_op jit(solution)/shard_map/decode/pallas_call | solution.py:471
where the time goes:
time: 43.9 us; the launch traced here: 43.6 us
  Pallas kernels  43 us (98%)
  between operations  0.64 us (1%)
    pallas_call x1, Pallas kernels, encode(): pl.pallas_call(functools.partial(encoder_kernel, peers), name='encode', o...  34.1 us
    pallas_call x1, Pallas kernels, decode(): pl.pallas_call(decoder_kernel, name='decode', out_shape=(jax.ShapeDtypeSt...  8.86 us

commit v1 on v0

v1 whole, which is shorter than its diff:
```python
import functools
import math

import jax
import jax.numpy as jnp
from jax import lax
from jax.experimental import pallas as pl
from jax.experimental.pallas import tpu as pltpu
from jax.sharding import PartitionSpec as P

HEADS = 8
norm_eps = 1e-06
F32 = jnp.float32
BF16 = jnp.bfloat16


def rms_norm(values, weight_gain):
    widened = values.astype(F32)
    spread = jnp.mean(widened * widened, axis=-1, keepdims=True)
    return (widened * lax.rsqrt(spread + norm_eps) * weight_gain).astype(BF16)


def attend_dense(queries, pairs, edges):
    rows, width = queries.shape
    head = width // HEADS
    q = queries.reshape(rows, HEADS, head)
    k = pairs[:, :width].reshape(-1, HEADS, head)
    v = pairs[:, width:].reshape(-1, HEADS, head)
    scores = jnp.einsum("rhd,khd->hrk", q, k, preferred_element_type=F32)
    scores = jnp.where(edges[None] > 0, scores * (1.0 / math.sqrt(head)), -1e30)
    highest = jnp.max(scores, axis=-1, keepdims=True)
    raised = jnp.exp(scores - highest) * edges[None]
    weights = (raised / jnp.sum(raised, axis=-1, keepdims=True)).astype(BF16)
    mixed = jnp.einsum("hrk,khd->rhd", weights, v, preferred_element_type=F32)
    return mixed.reshape(rows, width).astype(BF16)


def on_device(grid, latent_in, grid_gain, node_gain, dec_gain, w_q_enc, w_kv_enc, w_o_enc,
              w_q_dec, w_kv_dec, w_o_dec, enc_need, enc_slot, enc_count, dec_need, dec_slot):
    peers = lax.axis_size("dom")
    nodes = latent_in.shape[0]
    normed_grid = rms_norm(grid, grid_gain)
    wanted = lax.all_to_all(enc_need.reshape(peers, -1), "dom", split_axis=0, concat_axis=0, tiled=True)
    band = jnp.arange(grid.shape[0], dtype=jnp.int32)
    pick = (wanted.reshape(-1)[:, None] == band[None, :]).astype(BF16)
    chosen = jnp.dot(pick, normed_grid, preferred_element_type=F32).astype(BF16)
    rows = jnp.dot(chosen, w_kv_enc, preferred_element_type=F32).astype(BF16)
    arrived = lax.all_to_all(rows, "dom", split_axis=0, concat_axis=0, tiled=True)
    enc_queries = jnp.dot(rms_norm(latent_in, node_gain), w_q_enc, preferred_element_type=F32).astype(BF16)
    live = jnp.arange(enc_slot.shape[0], dtype=jnp.int32)[:, None] < enc_count[None, :]
    slot_row = jnp.arange(enc_need.shape[1], dtype=jnp.int32)
    enc_edges = jnp.sum((live[:, :, None] & (enc_slot[:, :, None] == slot_row)).astype(F32), axis=0)
    enc_mixed = attend_dense(enc_queries, arrived, enc_edges)
    enc_update = jnp.dot(enc_mixed, w_o_enc, preferred_element_type=F32)
    latent_out = (latent_in.astype(F32) + enc_update).astype(BF16)
    latent_pairs = jnp.dot(rms_norm(latent_out, dec_gain), w_kv_dec, preferred_element_type=F32).astype(BF16)
    dec_queries = jnp.dot(normed_grid, w_q_dec, preferred_element_type=F32).astype(BF16)
    everyone = lax.all_gather(latent_pairs, "dom", axis=0, tiled=True)
    total = dec_need.shape[1]
    cap = total // peers
    lanes = 128
    table = dec_need.reshape(total // lanes, lanes).astype(BF16)
    high = (dec_slot // lanes)[:, :, None] == jnp.arange(total // lanes, dtype=jnp.int32)
    low = (dec_slot % lanes)[:, :, None] == jnp.arange(lanes, dtype=jnp.int32)
    need = jnp.einsum("jgt,tl->jgl", high.astype(BF16), table, preferred_element_type=F32)
    need = jnp.sum(jnp.where(low, need, 0.0), axis=-1).astype(jnp.int32)
    node = (dec_slot // cap) * nodes + need
    dec_edges = jnp.sum((node[:, :, None] == jnp.arange(peers * nodes, dtype=jnp.int32)).astype(F32), axis=0)
    dec_mixed = attend_dense(dec_queries, everyone, dec_edges)
    dec_update = jnp.dot(dec_mixed, w_o_dec, preferred_element_type=F32)
    grid_out = (grid.astype(F32) + dec_update).astype(BF16)
    return (latent_out, grid_out)


NT = (((1,), (1,)), ((), ()))
TN = (((0,), (0,)), ((), ()))
HIGH = lax.Precision.HIGHEST


def iota(shape, dim):
    return lax.broadcasted_iota(jnp.int32, shape, dim)


def norm_into(values, gain):
    widened = values.astype(F32)
    spread = jnp.mean(widened * widened, axis=-1, keepdims=True)
    return (widened * lax.rsqrt(spread + norm_eps) * gain).astype(BF16)


def encoder_kernel(
    peers, grid_hbm, latent_hbm, ggain_hbm, ngain_hbm, dgain_hbm, wq_hbm, wkv_hbm, wo_hbm, wqd_hbm, wkvd_hbm,
    need_hbm, slot_hbm, count_hbm, dslot_hbm, table_hbm,
    latent_hbm_out, pairs_hbm, queries_hbm, bias_hbm,
    grid_v, latent_v, ggain_v, ngain_v, dgain_v, wq_v, wkv_v, wo_v, wqd_v, wkvd_v, need_v, slot_v, count_v, dslot_v,
    table_v, normed, chosen, rows, fan_of, query_mine, edges_mine,
    need_all, query_all, edges_all, mix_send, stat_send, mix_all, stat_all, pairs_all,
    latent_new, queries_out, bias_out, node_of, worth_of, load_sem, store_sem, send_sem, recv_sem, push_send, push_recv,
):
    me = lax.axis_index("dom")
    nodes, model = latent_v.shape
    width = wq_v.shape[1]
    head = width // HEADS
    cap = need_v.shape[1] // peers
    group = 128 // cap
    chips = peers // 2
    side = lax.rem(me, 2)
    partner = me + 1 - 2 * side
    points = grid_v.shape[0]
    lanes = HEADS * nodes
    both = 2 * cap
    blocks = push_send.shape[0]
    block = points // blocks

    barrier = pltpu.get_barrier_semaphore()
    for to in [lax.rem(me + 2 * step, peers) for step in range(1, chips)] + [partner]:
        pl.semaphore_signal(barrier, inc=1, device_id={"dom": to}, device_id_type=pl.DeviceIdType.MESH)

    def block_at(number):
        return slice(number * block, (number + 1) * block)

    pairs_of_refs = {
        "slot": (slot_hbm, slot_v), "count": (count_hbm, count_v), "need": (need_hbm, need_v),
        "latent": (latent_hbm, latent_v), "ngain": (ngain_hbm, ngain_v), "wq": (wq_hbm, wq_v),
        "ggain": (ggain_hbm, ggain_v),
    }
    for number in range(blocks):
        pairs_of_refs[number] = (grid_hbm.at[block_at(number)], grid_v.at[block_at(number)])
    pairs_of_refs.update({
        "wkv": (wkv_hbm, wkv_v), "wqd": (wqd_hbm, wqd_v), "dslot": (dslot_hbm, dslot_v), "table": (table_hbm, table_v),
        "wo": (wo_hbm, wo_v), "dgain": (dgain_hbm, dgain_v), "wkvd": (wkvd_hbm, wkvd_v),
    })
    loads = {}
    for number, (name, (source, target)) in enumerate(pairs_of_refs.items()):
        loads[name] = pltpu.make_async_copy(source, target, load_sem.at[number])
        loads[name].start()

    def message(kind, source, target, to, leaving, landing):
        return pltpu.make_async_remote_copy(
            src_ref=source,
            dst_ref=target,
            send_sem=send_sem.at[kind, leaving],
            recv_sem=recv_sem.at[kind, landing],
            device_id={"dom": to},
            device_id_type=pl.DeviceIdType.MESH,
        )

    def chip(step):
        return lax.rem(me + 2 * step, peers)

    def need_to(step, slot):
        return message(0, need_v, need_all.at[slot], chip(step), step, slot)

    def edges_to(step, slot):
        return message(1, edges_mine.at[chip(step) // group], edges_all.at[slot], chip(step), step, slot)

    def query_to(step, slot):
        return message(2, query_mine, query_all.at[slot], chip(step), step, slot)

    def mix_to(step, slot):
        return message(3, mix_send.at[step], mix_all.at[slot], chip(step), step, slot)

    def stat_to(step, slot):
        return message(4, stat_send.at[step], stat_all.at[slot], chip(step), step, slot)

    def pairs_to(step, slot):
        return message(5, pairs_all.at[me], pairs_all.at[me], chip(step), step, slot)

    def pairs_on(step, slot):
        owner = chip(step)
        return message(6, pairs_all.at[owner], pairs_all.at[owner], partner, step, slot)

    def push(number):
        return pltpu.make_async_remote_copy(
            src_ref=normed.at[0, block_at(number)],
            dst_ref=normed.at[1, block_at(number)],
            send_sem=push_send.at[number],
            recv_sem=push_recv.at[number],
            device_id={"dom": partner},
            device_id_type=pl.DeviceIdType.MESH,
        )

    others = range(1, chips)

    loads["slot"].wait()
    loads["count"].wait()
    edge_total = slot_v.shape[1]
    own = iota((nodes, nodes), 0) == iota((nodes, nodes), 1)
    counts = jnp.sum(jnp.where(own, count_v[...].astype(F32), 0.0), axis=1, keepdims=True)
    slots = jnp.where(iota(slot_v.shape, 1).astype(F32) < counts, slot_v[...], -1)
    entry = iota((nodes, peers * cap), 1)
    tally = jnp.zeros((nodes, peers * cap), F32)
    for j in range(edge_total):
        tally = tally + jnp.where(slots[:, j : j + 1] == entry, 1.0, 0.0)
    tally = tally.astype(BF16)
    for part in range(peers // group):
        edges_mine[part] = tally[:, part * 128 : (part + 1) * 128]
    edges_all[0] = edges_mine[me // group]
    fan_row = iota((chips * nodes, chips * lanes), 0)
    fan_lane = iota((chips * nodes, chips * lanes), 1)
    fan = fan_row == (fan_lane // lanes) * nodes + lax.rem(fan_lane, nodes)
    fan_of[...] = jnp.where(fan, 1.0, 0.0).astype(BF16)
    loads["need"].wait()
    need_all[0] = need_v[...]
    loads["latent"].wait()
    loads["ngain"].wait()
    loads["wq"].wait()
    queries = jnp.dot(
        norm_into(latent_v[...], ngain_v[...]), wq_v[...], preferred_element_type=F32
    ).astype(BF16)
    query_mine[...] = queries
    query_all[0] = queries

    pl.semaphore_wait(barrier, chips)
    for step in others:
        need_to(step, chips - step).start()
    for step in others:
        edges_to(step, chips - step).start()
        query_to(step, chips - step).start()

    loads["ggain"].wait()
    for number in range(blocks):
        loads[number].wait()

        def norm_block(piece, carry):
            at = pl.ds(pl.multiple_of(number * block + piece * 128, 128), 128)
            normed[0, at, :] = norm_into(grid_v[at, :], ggain_v[...])
            return carry

        lax.fori_loop(0, block // 128, norm_block, 0)
        push(number).start()

    for step in others:
        need_to(step, step).wait_recv()
    base = pl.multiple_of((me // group) * 128, 128)
    lists = need_all[:, :, pl.ds(base, 128)]
    within = lax.rem(me // 2, group // 2) * both
    asked = jnp.broadcast_to(lists, (chips, cap, 128)).astype(F32)
    spot = iota((chips, cap, 128), 1)
    lane = iota((chips, cap, 128), 2)
    wanted = []
    for band in (side, 1 - side):
        picked = jnp.where(lane == within + band * cap + spot, asked, 0.0)
        wanted.append(jnp.sum(picked, axis=2, keepdims=True).astype(jnp.int32).reshape(chips * cap, 1))
    point = iota((chips * cap, points), 1)
    pick = jnp.where(wanted[0] == point, 1.0, 0.0).astype(BF16)
    chosen[: chips * cap] = jnp.dot(pick, normed[0], preferred_element_type=F32).astype(BF16)
    pick = jnp.where(wanted[1] == point, 1.0, 0.0).astype(BF16)
    for number in range(blocks):
        push(number).wait_recv()
    chosen[chips * cap :] = jnp.dot(pick, normed[1], preferred_element_type=F32).astype(BF16)
    loads["wkv"].wait()
    rows[...] = jnp.dot(chosen[...], wkv_v[...], preferred_element_type=F32).astype(BF16)

    for step in others:
        edges_to(step, step).wait_recv()
    spot = iota((both, 128), 0)
    band = jnp.where(spot < cap, side, 1 - side)
    mine = iota((both, 128), 1) == within + band * cap + lax.rem(spot, cap)
    entries = lax.dot_general(
        jnp.where(mine, 1.0, 0.0).astype(BF16), edges_all[...].reshape(chips * nodes, 128), NT,
        preferred_element_type=F32,
    ).astype(BF16)
    entries = jnp.dot(entries, fan_of[...], preferred_element_type=F32)
    for step in others:
        query_to(step, step).wait_recv()

    own_head = iota((lanes, width), 0) // nodes == iota((lanes, width), 1) // head

    def window(w):
        spread_query = jnp.broadcast_to(query_all[w][None], (HEADS, nodes, width)).reshape(lanes, width)
        spread_query = jnp.where(own_head, spread_query, jnp.zeros_like(spread_query))
        near = slice(w * cap, (w + 1) * cap)
        far = slice((chips + w) * cap, (chips + w + 1) * cap)
        keys_here = jnp.concatenate([rows[near, :width], rows[far, :width]], axis=0)
        values_here = jnp.concatenate([rows[near, width:], rows[far, width:]], axis=0)
        scores = lax.dot_general(keys_here, spread_query, NT, preferred_element_type=F32)
        times = entries[:, w * lanes : (w + 1) * lanes]
        scores = jnp.where(times > 0, scores * (1.0 / math.sqrt(head)), -1e30)
        highest = jnp.max(scores, axis=0, keepdims=True)
        raised = jnp.exp(scores - highest) * times
        total = jnp.sum(raised, axis=0, keepdims=True)
        mixed = lax.dot_general(raised.astype(BF16), values_here, TN, preferred_element_type=F32)
        mixed = jnp.where(own_head, mixed, 0.0).reshape(HEADS, nodes, width)
        return jnp.sum(mixed, axis=0).astype(BF16), highest, total

    for step, answer in [(step, window(step)) for step in range(chips)]:
        mixes, stats = (mix_all, stat_all) if step == 0 else (mix_send, stat_send)
        mixes[step] = answer[0]
        stats[step, 0:1, :] = answer[1]
        stats[step, 1:2, :] = answer[2]
    for step in others:
        mix_to(step, chips - step).start()
        stat_to(step, chips - step).start()

    loads["wqd"].wait()
    scale = math.log2(math.e) / math.sqrt(head)
    queries_out[...] = (jnp.dot(normed[0], wqd_v[...], preferred_element_type=F32) * scale).astype(BF16)
    queries_store = pltpu.make_async_copy(queries_out, queries_hbm, store_sem.at[0])
    queries_store.start()

    loads["dslot"].wait()
    loads["table"].wait()
    keys = peers * nodes
    dec_cap = table_v.shape[0] * 128 // peers
    slots = dslot_v[...]
    edge_total = slots.shape[0]
    slots = jnp.concatenate([slots] * (8 // edge_total), axis=0)
    columns = []
    for part in range(points // 128):
        piece = slots[:, part * 128 : (part + 1) * 128]
        high = piece // 128
        low = lax.rem(piece, 128)
        need = jnp.zeros_like(piece)
        for line in range(table_v.shape[0]):
            entry = jnp.broadcast_to(table_v[line : line + 1, :], piece.shape)
            need = jnp.where(high == line, jnp.take_along_axis(entry, low, axis=1), need)
        columns.append((piece // dec_cap) * nodes + need)
    node = jnp.concatenate(columns, axis=1)
    times = jnp.ones(node.shape, F32)
    for j in range(1, edge_total):
        times = times + jnp.where(node == jnp.concatenate([node[j:], node[:j]], axis=0), 1.0, 0.0)
    node_of[...] = node.astype(F32).T
    worth_of[...] = jnp.log2(times).T
    name = iota((128, keys), 1).astype(F32)

    def bias_block(piece, carry):
        at = pl.ds(pl.multiple_of(piece * 128, 128), 128)
        nodes_here, worth_here = node_of[at, :], worth_of[at, :]
        bias = jnp.full((128, keys), -1e30, F32)
        for j in range(edge_total):
            bias = jnp.where(nodes_here[:, j : j + 1] == name, worth_here[:, j : j + 1], bias)
        bias_out[at, :] = bias
        return carry

    lax.fori_loop(0, points // 128, bias_block, 0)
    bias_store = pltpu.make_async_copy(bias_out, bias_hbm, store_sem.at[1])
    bias_store.start()
    loads["wo"].wait()
    loads["dgain"].wait()
    loads["wkvd"].wait()

    for step in others:
        stat_to(step, step).wait_recv()
    tops = [stat_all[step, 0:1, :] for step in range(chips)]
    sums = [stat_all[step, 1:2, :] for step in range(chips)]
    top = functools.reduce(jnp.maximum, tops)
    shares = [jnp.exp(one - top) for one in tops]
    whole = functools.reduce(jnp.add, [a * b for a, b in zip(shares, sums)])
    own_node = iota((nodes, lanes), 0) == lax.rem(iota((nodes, lanes), 1), nodes)
    stacked = jnp.concatenate([jnp.where(own_node, share / whole, 0.0) for share in shares], axis=0)
    widen = (iota((lanes, width), 0) // nodes == iota((lanes, width), 1) // head).astype(F32)
    factors = jnp.dot(stacked, widen, precision=HIGH, preferred_element_type=F32).reshape(chips, nodes, width)
    for step in others:
        mix_to(step, step).wait_recv()
    enc_mixed = jnp.sum(factors * mix_all[...].astype(F32), axis=0).astype(BF16)
    update = jnp.dot(enc_mixed, wo_v[...], preferred_element_type=F32)
    fresh = (latent_v[...].astype(F32) + update).astype(BF16)
    latent_new[...] = fresh
    latent_store = pltpu.make_async_copy(latent_new, latent_hbm_out, store_sem.at[2])
    latent_store.start()
    pairs = jnp.dot(norm_into(fresh, dgain_v[...]), wkvd_v[...], preferred_element_type=F32).astype(BF16)
    pairs_all[me] = pairs
    for step in others:
        pairs_to(step, chips - step).start()
    pairs_near = message(6, pairs_all.at[me], pairs_all.at[me], partner, 0, 0)
    pairs_near.start()

    for step in others:
        pairs_to(step, step).wait_recv()
        pairs_on(step, step).start()
    pairs_near.wait_recv()
    for step in others:
        pairs_on(step, step).wait_recv()
    pairs_store = pltpu.make_async_copy(pairs_all, pairs_hbm, store_sem.at[3])
    pairs_store.start()

    for step in others:
        for outgoing in (need_to, edges_to, query_to, mix_to, stat_to, pairs_to, pairs_on):
            outgoing(step, step).wait_send()
    pairs_near.wait_send()
    for number in range(blocks):
        push(number).wait_send()
    queries_store.wait()
    bias_store.wait()
    latent_store.wait()
    pairs_store.wait()


BLOCKS = 4


def encode(grid, latent_in, grid_gain, node_gain, dec_gain, w_q_enc, w_kv_enc, w_o_enc, w_q_dec, w_kv_dec,
           enc_need, enc_slot, enc_count, dec_slot, dec_need):
    peers = lax.axis_size("dom")
    nodes, model = latent_in.shape
    width = w_q_enc.shape[1]
    entries = enc_need.shape[1]
    cap = entries // peers
    points = grid.shape[0]
    chips = peers // 2
    lanes = HEADS * nodes
    far = pl.BlockSpec(memory_space=pl.ANY)
    operands = (grid, latent_in, grid_gain[None], node_gain[None], dec_gain[None], w_q_enc, w_kv_enc, w_o_enc, w_q_dec,
                w_kv_dec, enc_need, enc_slot.T, enc_count[None], dec_slot, dec_need.reshape(-1, 128))
    latent_out, pairs, queries, bias = pl.pallas_call(
        functools.partial(encoder_kernel, peers),
        name="encode",
        out_shape=(
            jax.ShapeDtypeStruct((nodes, model), BF16),
            jax.ShapeDtypeStruct((peers, nodes, 2 * width), BF16),
            jax.ShapeDtypeStruct((points, width), BF16),
            jax.ShapeDtypeStruct((points, peers * nodes), F32),
        ),
        in_specs=[far] * len(operands),
        out_specs=(far,) * 4,
        scratch_shapes=[pltpu.VMEM(one.shape, one.dtype) for one in operands] + [
            pltpu.VMEM((2, points, model), BF16),
            pltpu.VMEM((entries, model), BF16),
            pltpu.VMEM((entries, 2 * width), BF16),
            pltpu.VMEM((chips * nodes, chips * lanes), BF16),
            pltpu.VMEM((nodes, width), BF16),
            pltpu.VMEM((entries // 128, nodes, 128), BF16),
            pltpu.VMEM((chips, 1, entries), jnp.int32),
            pltpu.VMEM((chips, nodes, width), BF16),
            pltpu.VMEM((chips, nodes, 128), BF16),
            pltpu.VMEM((chips, nodes, width), BF16),
            pltpu.VMEM((chips, 2, lanes), F32),
            pltpu.VMEM((chips, nodes, width), BF16),
            pltpu.VMEM((chips, 2, lanes), F32),
            pltpu.VMEM((peers, nodes, 2 * width), BF16),
            pltpu.VMEM((nodes, model), BF16),
            pltpu.VMEM((points, width), BF16),
            pltpu.VMEM((points, peers * nodes), F32),
            pltpu.VMEM((points, 8), F32),
            pltpu.VMEM((points, 8), F32),
            pltpu.SemaphoreType.DMA((len(operands) - 1 + BLOCKS,)),
            pltpu.SemaphoreType.DMA((4,)),
            pltpu.SemaphoreType.DMA((7, chips)),
            pltpu.SemaphoreType.DMA((7, chips)),
            pltpu.SemaphoreType.DMA((BLOCKS,)),
            pltpu.SemaphoreType.DMA((BLOCKS,)),
        ],
        compiler_params=pltpu.CompilerParams(
            collective_id=0, has_side_effects=True, vmem_limit_bytes=60 * 1024 * 1024
        ),
    )(*operands)
    return latent_out, pairs.reshape(peers * nodes, 2 * width), queries, bias


def decoder_kernel(query_hbm, pairs_hbm, bias_hbm, grid_hbm, wo_hbm, latent_ref, out_hbm, latent_out,
                   query_v, pairs_v, bias_v, grid_v, wo_v, out_v, keys_of, values_of, mixed, load_sem, store_sem):
    points, width = query_v.shape
    head = width // HEADS
    keys = pairs_v.shape[0]
    quad = 4
    chunks = CHUNKS
    tile = points // chunks

    def rows(part):
        return slice(part * tile, (part + 1) * tile)

    load_pairs = pltpu.make_async_copy(pairs_hbm, pairs_v, load_sem.at[0])
    load_wo = pltpu.make_async_copy(wo_hbm, wo_v, load_sem.at[1])
    load_query = [
        pltpu.make_async_copy(query_hbm.at[rows(part)], query_v.at[rows(part)], load_sem.at[2 + part])
        for part in range(chunks)
    ]
    load_bias = [
        pltpu.make_async_copy(bias_hbm.at[rows(part)], bias_v.at[rows(part)], load_sem.at[2 + chunks + part])
        for part in range(chunks)
    ]
    load_grid = pltpu.make_async_copy(grid_hbm, grid_v, load_sem.at[2 + 2 * chunks])
    load_pairs.start()
    for part in range(chunks):
        load_query[part].start()
        load_bias[part].start()
    load_wo.start()
    load_grid.start()

    latent_out[...] = latent_ref[...]
    load_pairs.wait()
    lane_head = iota((keys, quad * head), 1) // head
    for h in range(HEADS):
        some = pairs_v[:, (h // quad) * quad * head : (h // quad + 1) * quad * head]
        keys_of[h] = jnp.where(lane_head == h % quad, some, jnp.zeros_like(some))
    side_of = iota((keys, 2 * head), 1) // head
    for pair in range(HEADS // 2):
        some = pairs_v[:, width + pair * 2 * head : width + (pair + 1) * 2 * head]
        for side in range(2):
            own = side_of == side
            at = slice(side * keys, (side + 1) * keys)
            values_of[pair, at, : 2 * head] = jnp.where(own, some, jnp.zeros_like(some))
            values_of[pair, at, 2 * head :] = jnp.where(own, jnp.ones_like(some), jnp.zeros_like(some))

    stores = []
    for part in range(chunks):
        at = rows(part)
        load_query[part].wait()
        load_bias[part].wait()
        for pair in range(HEADS // 2):
            four = 2 * pair // quad
            query = query_v[at, four * quad * head : (four + 1) * quad * head]
            raised = []
            for side in range(2):
                scores = lax.dot_general(query, keys_of[2 * pair + side], NT, preferred_element_type=F32)
                scores = scores + bias_v[at, :]
                highest = jnp.max(scores, axis=1, keepdims=True)
                raised.append(jnp.exp2(scores - highest).astype(BF16))
            got = jnp.dot(jnp.concatenate(raised, axis=1), values_of[pair], preferred_element_type=F32)
            mixed[at, pair * 2 * head : (pair + 1) * 2 * head] = (got[:, : 2 * head] / got[:, 2 * head :]).astype(BF16)
        if part == 0:
            load_wo.wait()
            load_grid.wait()
        update = jnp.dot(mixed[at, :], wo_v[...], preferred_element_type=F32)
        out_v[at, :] = (grid_v[at, :].astype(F32) + update).astype(BF16)
        stores.append(pltpu.make_async_copy(out_v.at[at], out_hbm.at[at], store_sem.at[part]))
        stores[-1].start()
    for store in stores:
        store.wait()


CHUNKS = 2


def decode(queries, pairs, bias, grid, w_o_dec, latent_out):
    points, model = grid.shape
    width = queries.shape[1]
    keys = pairs.shape[0]
    vmem = pl.BlockSpec(memory_space=pltpu.VMEM)
    far = pl.BlockSpec(memory_space=pl.ANY)
    return pl.pallas_call(
        decoder_kernel,
        name="decode",
        out_shape=(
            jax.ShapeDtypeStruct(grid.shape, BF16),
            jax.ShapeDtypeStruct(latent_out.shape, BF16),
        ),
        in_specs=[far, far, far, far, far, vmem],
        out_specs=(far, vmem),
        scratch_shapes=[
            pltpu.VMEM(queries.shape, BF16),
            pltpu.VMEM(pairs.shape, BF16),
            pltpu.VMEM(bias.shape, F32),
            pltpu.VMEM(grid.shape, BF16),
            pltpu.VMEM(w_o_dec.shape, BF16),
            pltpu.VMEM(grid.shape, BF16),
            pltpu.VMEM((HEADS, keys, width // 2), BF16),
            pltpu.VMEM((HEADS // 2, 2 * keys, 4 * width // HEADS), BF16),
            pltpu.VMEM((points, width), BF16),
            pltpu.SemaphoreType.DMA((3 + 2 * CHUNKS,)),
            pltpu.SemaphoreType.DMA((CHUNKS,)),
        ],
    )(queries, pairs, bias, grid, w_o_dec, latent_out)


def by_kernels(grid, latent_in, grid_gain, node_gain, dec_gain, w_q_enc, w_kv_enc, w_o_enc,
               w_q_dec, w_kv_dec, w_o_dec, enc_need, enc_slot, enc_count, dec_need, dec_slot):
    latent_out, pairs, queries, bias = encode(
        grid, latent_in, grid_gain, node_gain, dec_gain, w_q_enc, w_kv_enc, w_o_enc, w_q_dec, w_kv_dec,
        enc_need, enc_slot, enc_count, dec_slot, dec_need)
    grid_out, latent_out = decode(queries, pairs, bias, grid, w_o_dec, latent_out)
    return (latent_out, grid_out)


def chosen_form(*args):
    grid, latent_in, enc_need, dec_slot = args[0], args[1], args[11], args[15]
    peers = lax.axis_size("dom")
    cap = enc_need.shape[1] // peers
    small = latent_in.shape[0] * peers <= 256
    fits = peers % 2 == 0 and 128 % cap == 0 and cap in (32, 64) and HEADS * latent_in.shape[0] == 128 and grid.shape[0] % 512 == 0
    if small and fits and 8 % dec_slot.shape[0] == 0:
        return by_kernels(*args)
    return on_device(*args)


def solution(mesh):
    both, rep = P(("groups", "dom"), None), P()
    return jax.shard_map(
        chosen_form,
        mesh=mesh,
        in_specs=(both, both, *([rep] * 9), P("dom", None), P(None, "dom"), P("dom"), P("dom", None), P(None, "dom")),
        out_specs=(both, both),
        check_vma=False,
    )
```

time: 43.9 us -> 38.7 us (0.88)
  Pallas kernels: 43 us -> 37.9 us
    pallas_call x1, Pallas kernels: 34.1 us -> 29.8 us  [encode(): pl.pallas_call(functools.partial(encoder_kernel, peers), name='encode', o...]
    pallas_call x1, Pallas kernels: 8.86 us -> 8.07 us  [decode(): pl.pallas_call(decoder_kernel, name='decode', out_shape=(jax.ShapeDtypeSt...]
where the time goes in v1:
time: 38.7 us; the launch traced here: 38.5 us
  Pallas kernels  37.9 us (98%)
  between operations  0.64 us (2%)
    pallas_call x1, Pallas kernels, encode(): pl.pallas_call(functools.partial(encoder_kernel, peers), name='encode', o...  29.8 us
    pallas_call x1, Pallas kernels, decode(): pl.pallas_call(decoder_kernel, name='decode', out_shape=(jax.ShapeDtypeSt...  8.07 us

profile of v1, /device:TPU:1, one launch (start us, length us, event | category | flops | bytes accessed | tf_op | source)
XLA Modules:
  0.0 38.5 jit_solution(17944584137884582838)
XLA Ops:
  0.6 29.8 %encode.1 = (bf16[16,1024]{1,0:T(8,128)(2,1)}, bf16[16,16,1024]{2,1,0:T(8,128)(2,1)}, bf16[1024,512]{1,0:T(8,128)(2,1)}, f32[1024,256]{1,0:T(8,128)}) custom-call(bf16[1024,1024]{1,0:T(8,128)(2,1)} %grid_hbm.3, bf16[16,1024]{1,0:T(8,128)(2,1)} %latent_hbm.1, f32[1,1024]{1,0:T(1,128)} %bitcast.10, f32[1,1024]{1,0:T(1,128)} %bitcast.11, f32[1,1024]{1,0:T(1,128)} %bitcast.12, ...), custom_call_target="tpu_custom_call" | custom-call | tf_op jit(solution)/shard_map/encode/pallas_call | solution.py:405
  30.4 8.1 %decode.1 = (bf16[1024,1024]{1,0:T(8,128)(2,1)}, bf16[16,1024]{1,0:T(8,128)(2,1)}) custom-call(bf16[1024,512]{1,0:T(8,128)(2,1)} %get-tuple-element.8.query_hbm, bf16[256,1024]{1,0:T(8,128)(2,1)} %bitcast.7, f32[1024,256]{1,0:T(8,128)} %get-tuple-element.10.bias_hbm, bf16[1024,1024]{1,0:T(8,128)(2,1)} %grid_hbm.3, bf16[512,1024]{1,0:T(8,128)(2,1)} %wo_hbm.3, ...), custom_call_target="tpu_custom_call" | custom-call | tf_op jit(solution)/shard_map/decode/pallas_call | solution.py:531

commit v2 on v1

--- a/solution.py
+++ b/solution.py
@@ -89,12 +89,12 @@
 
 def encoder_kernel(
     peers, grid_hbm, latent_hbm, ggain_hbm, ngain_hbm, dgain_hbm, wq_hbm, wkv_hbm, wo_hbm, wqd_hbm, wkvd_hbm,
-    need_hbm, slot_hbm, count_hbm, dslot_hbm, table_hbm,
-    latent_hbm_out, pairs_hbm, queries_hbm, bias_hbm,
-    grid_v, latent_v, ggain_v, ngain_v, dgain_v, wq_v, wkv_v, wo_v, wqd_v, wkvd_v, need_v, slot_v, count_v, dslot_v,
+    need_hbm, slot_hbm, count_hbm, dslot_hbm, table_hbm, wod_hbm,
+    latent_new, pairs_out, queries_out, bias_out, grid_v, wod_v,
+    latent_v, ggain_v, ngain_v, dgain_v, wq_v, wkv_v, wo_v, wqd_v, wkvd_v, need_v, slot_v, count_v, dslot_v,
     table_v, normed, chosen, rows, fan_of, query_mine, edges_mine,
     need_all, query_all, edges_all, mix_send, stat_send, mix_all, stat_all, pairs_all,
-    latent_new, queries_out, bias_out, node_of, worth_of, load_sem, store_sem, send_sem, recv_sem, push_send, push_recv,
+    node_of, worth_of, load_sem, send_sem, recv_sem, push_send, push_recv,
 ):
     me = lax.axis_index("dom")
     nodes, model = latent_v.shape
@@ -127,7 +127,7 @@
         pairs_of_refs[number] = (grid_hbm.at[block_at(number)], grid_v.at[block_at(number)])
     pairs_of_refs.update({
         "wkv": (wkv_hbm, wkv_v), "wqd": (wqd_hbm, wqd_v), "dslot": (dslot_hbm, dslot_v), "table": (table_hbm, table_v),
-        "wo": (wo_hbm, wo_v), "dgain": (dgain_hbm, dgain_v), "wkvd": (wkvd_hbm, wkvd_v),
+        "wo": (wo_hbm, wo_v), "dgain": (dgain_hbm, dgain_v), "wkvd": (wkvd_hbm, wkvd_v), "wod": (wod_hbm, wod_v),
     })
     loads = {}
     for number, (name, (source, target)) in enumerate(pairs_of_refs.items()):
@@ -295,8 +295,6 @@
     loads["wqd"].wait()
     scale = math.log2(math.e) / math.sqrt(head)
     queries_out[...] = (jnp.dot(normed[0], wqd_v[...], preferred_element_type=F32) * scale).astype(BF16)
-    queries_store = pltpu.make_async_copy(queries_out, queries_hbm, store_sem.at[0])
-    queries_store.start()
 
     loads["dslot"].wait()
     loads["table"].wait()
@@ -333,8 +331,6 @@
         return carry
 
     lax.fori_loop(0, points // 128, bias_block, 0)
-    bias_store = pltpu.make_async_copy(bias_out, bias_hbm, store_sem.at[1])
-    bias_store.start()
     loads["wo"].wait()
     loads["dgain"].wait()
     loads["wkvd"].wait()
@@ -356,8 +352,6 @@
     update = jnp.dot(enc_mixed, wo_v[...], preferred_element_type=F32)
     fresh = (latent_v[...].astype(F32) + update).astype(BF16)
     latent_new[...] = fresh
-    latent_store = pltpu.make_async_copy(latent_new, latent_hbm_out, store_sem.at[2])
-    latent_store.start()
     pairs = jnp.dot(norm_into(fresh, dgain_v[...]), wkvd_v[...], preferred_element_type=F32).astype(BF16)
     pairs_all[me] = pairs
     for step in others:
@@ -371,8 +365,7 @@
     pairs_near.wait_recv()
     for step in others:
         pairs_on(step, step).wait_recv()
-    pairs_store = pltpu.make_async_copy(pairs_all, pairs_hbm, store_sem.at[3])
-    pairs_store.start()
+    pairs_out[...] = pairs_all[...].reshape(pairs_out.shape)
 
     for step in others:
         for outgoing in (need_to, edges_to, query_to, mix_to, stat_to, pairs_to, pairs_on):
@@ -380,16 +373,16 @@
     pairs_near.wait_send()
     for number in range(blocks):
         push(number).wait_send()
-    queries_store.wait()
-    bias_store.wait()
-    latent_store.wait()
-    pairs_store.wait()
+    loads["wod"].wait()
 
 
 BLOCKS = 4
 
 
-def encode(grid, latent_in, grid_gain, node_gain, dec_gain, w_q_enc, w_kv_enc, w_o_enc, w_q_dec, w_kv_dec,
+VMEM_LIMIT = 32 * 1024 * 1024
+
+
+def encode(grid, latent_in, grid_gain, node_gain, dec_gain, w_q_enc, w_kv_enc, w_o_enc, w_q_dec, w_kv_dec, w_o_dec,
            enc_need, enc_slot, enc_count, dec_slot, dec_need):
     peers = lax.axis_size("dom")
     nodes, model = latent_in.shape
@@ -399,21 +392,24 @@
     points = grid.shape[0]
     chips = peers // 2
     lanes = HEADS * nodes
-    far = pl.BlockSpec(memory_space=pl.ANY)
+    far = pl.BlockSpec(memory_space=pltpu.HBM)
+    vmem = pl.BlockSpec(memory_space=pltpu.VMEM)
     operands = (grid, latent_in, grid_gain[None], node_gain[None], dec_gain[None], w_q_enc, w_kv_enc, w_o_enc, w_q_dec,
-                w_kv_dec, enc_need, enc_slot.T, enc_count[None], dec_slot, dec_need.reshape(-1, 128))
-    latent_out, pairs, queries, bias = pl.pallas_call(
+                w_kv_dec, enc_need, enc_slot.T, enc_count[None], dec_slot, dec_need.reshape(-1, 128), w_o_dec)
+    return pl.pallas_call(
         functools.partial(encoder_kernel, peers),
         name="encode",
         out_shape=(
-            jax.ShapeDtypeStruct((nodes, model), BF16),
-            jax.ShapeDtypeStruct((peers, nodes, 2 * width), BF16),
-            jax.ShapeDtypeStruct((points, width), BF16),
-            jax.ShapeDtypeStruct((points, peers * nodes), F32),
+            pltpu.VMEM((nodes, model), BF16),
+            pltpu.VMEM((peers * nodes, 2 * width), BF16),
+            pltpu.VMEM((points, width), BF16),
+            pltpu.VMEM((points, peers * nodes), F32),
+            pltpu.VMEM(grid.shape, BF16),
+            pltpu.VMEM(w_o_dec.shape, BF16),
         ),
         in_specs=[far] * len(operands),
-        out_specs=(far,) * 4,
-        scratch_shapes=[pltpu.VMEM(one.shape, one.dtype) for one in operands] + [
+        out_specs=(vmem,) * 6,
+        scratch_shapes=[pltpu.VMEM(one.shape, one.dtype) for one in operands[1:-1]] + [
             pltpu.VMEM((2, points, model), BF16),
             pltpu.VMEM((entries, model), BF16),
             pltpu.VMEM((entries, 2 * width), BF16),
@@ -428,27 +424,20 @@
             pltpu.VMEM((chips, nodes, width), BF16),
             pltpu.VMEM((chips, 2, lanes), F32),
             pltpu.VMEM((peers, nodes, 2 * width), BF16),
-            pltpu.VMEM((nodes, model), BF16),
-            pltpu.VMEM((points, width), BF16),
-            pltpu.VMEM((points, peers * nodes), F32),
             pltpu.VMEM((points, 8), F32),
             pltpu.VMEM((points, 8), F32),
             pltpu.SemaphoreType.DMA((len(operands) - 1 + BLOCKS,)),
-            pltpu.SemaphoreType.DMA((4,)),
             pltpu.SemaphoreType.DMA((7, chips)),
             pltpu.SemaphoreType.DMA((7, chips)),
             pltpu.SemaphoreType.DMA((BLOCKS,)),
             pltpu.SemaphoreType.DMA((BLOCKS,)),
         ],
-        compiler_params=pltpu.CompilerParams(
-            collective_id=0, has_side_effects=True, vmem_limit_bytes=60 * 1024 * 1024
-        ),
-    )(*operands)
-    return latent_out, pairs.reshape(peers * nodes, 2 * width), queries, bias
-
-
-def decoder_kernel(query_hbm, pairs_hbm, bias_hbm, grid_hbm, wo_hbm, latent_ref, out_hbm, latent_out,
-                   query_v, pairs_v, bias_v, grid_v, wo_v, out_v, keys_of, values_of, mixed, load_sem, store_sem):
+        compiler_params=pltpu.CompilerParams(collective_id=0, has_side_effects=True, vmem_limit_bytes=VMEM_LIMIT),
+    )(*[pltpu.with_memory_space_constraint(one, pltpu.HBM) for one in operands])
+
+
+def decoder_kernel(latent_ref, pairs_v, query_v, bias_v, grid_v, wo_v, latent_hbm, out_hbm,
+                   out_v, keys_of, values_of, mixed, store_sem):
     points, width = query_v.shape
     head = width // HEADS
     keys = pairs_v.shape[0]
@@ -459,26 +448,8 @@
     def rows(part):
         return slice(part * tile, (part + 1) * tile)
 
-    load_pairs = pltpu.make_async_copy(pairs_hbm, pairs_v, load_sem.at[0])
-    load_wo = pltpu.make_async_copy(wo_hbm, wo_v, load_sem.at[1])
-    load_query = [
-        pltpu.make_async_copy(query_hbm.at[rows(part)], query_v.at[rows(part)], load_sem.at[2 + part])
-        for part in range(chunks)
-    ]
-    load_bias = [
-        pltpu.make_async_copy(bias_hbm.at[rows(part)], bias_v.at[rows(part)], load_sem.at[2 + chunks + part])
-        for part in range(chunks)
-    ]
-    load_grid = pltpu.make_async_copy(grid_hbm, grid_v, load_sem.at[2 + 2 * chunks])
-    load_pairs.start()
-    for part in range(chunks):
-        load_query[part].start()
-        load_bias[part].start()
-    load_wo.start()
-    load_grid.start()
-
-    latent_out[...] = latent_ref[...]
-    load_pairs.wait()
+    stores = [pltpu.make_async_copy(latent_ref, latent_hbm, store_sem.at[chunks * PIECES])]
+    stores[0].start()
     lane_head = iota((keys, quad * head), 1) // head
     for h in range(HEADS):
         some = pairs_v[:, (h // quad) * quad * head : (h // quad + 1) * quad * head]
@@ -492,11 +463,8 @@
             values_of[pair, at, : 2 * head] = jnp.where(own, some, jnp.zeros_like(some))
             values_of[pair, at, 2 * head :] = jnp.where(own, jnp.ones_like(some), jnp.zeros_like(some))
 
-    stores = []
     for part in range(chunks):
         at = rows(part)
-        load_query[part].wait()
-        load_bias[part].wait()
         for pair in range(HEADS // 2):
             four = 2 * pair // quad
             query = query_v[at, four * quad * head : (four + 1) * quad * head]
@@ -508,58 +476,51 @@
                 raised.append(jnp.exp2(scores - highest).astype(BF16))
             got = jnp.dot(jnp.concatenate(raised, axis=1), values_of[pair], preferred_element_type=F32)
             mixed[at, pair * 2 * head : (pair + 1) * 2 * head] = (got[:, : 2 * head] / got[:, 2 * head :]).astype(BF16)
-        if part == 0:
-            load_wo.wait()
-            load_grid.wait()
-        update = jnp.dot(mixed[at, :], wo_v[...], preferred_element_type=F32)
-        out_v[at, :] = (grid_v[at, :].astype(F32) + update).astype(BF16)
-        stores.append(pltpu.make_async_copy(out_v.at[at], out_hbm.at[at], store_sem.at[part]))
-        stores[-1].start()
+        for piece in range(PIECES):
+            at = slice(part * tile + piece * (tile // PIECES), part * tile + (piece + 1) * (tile // PIECES))
+            update = jnp.dot(mixed[at, :], wo_v[...], preferred_element_type=F32)
+            out_v[at, :] = (grid_v[at, :].astype(F32) + update).astype(BF16)
+            stores.append(pltpu.make_async_copy(out_v.at[at], out_hbm.at[at], store_sem.at[part * PIECES + piece]))
+            stores[-1].start()
     for store in stores:
         store.wait()
 
 
 CHUNKS = 2
-
-
-def decode(queries, pairs, bias, grid, w_o_dec, latent_out):
+PIECES = 2
+
+
+def decode(latent_out, pairs, queries, bias, grid, w_o_dec):
     points, model = grid.shape
     width = queries.shape[1]
     keys = pairs.shape[0]
     vmem = pl.BlockSpec(memory_space=pltpu.VMEM)
-    far = pl.BlockSpec(memory_space=pl.ANY)
+    far = pl.BlockSpec(memory_space=pltpu.HBM)
     return pl.pallas_call(
         decoder_kernel,
         name="decode",
         out_shape=(
+            jax.ShapeDtypeStruct(latent_out.shape, BF16),
             jax.ShapeDtypeStruct(grid.shape, BF16),
-            jax.ShapeDtypeStruct(latent_out.shape, BF16),
         ),
-        in_specs=[far, far, far, far, far, vmem],
-        out_specs=(far, vmem),
+        in_specs=[vmem] * 6,
+        out_specs=(far, far),
         scratch_shapes=[
-            pltpu.VMEM(queries.shape, BF16),
-            pltpu.VMEM(pairs.shape, BF16),
-            pltpu.VMEM(bias.shape, F32),
-            pltpu.VMEM(grid.shape, BF16),
-            pltpu.VMEM(w_o_dec.shape, BF16),
             pltpu.VMEM(grid.shape, BF16),
             pltpu.VMEM((HEADS, keys, width // 2), BF16),
             pltpu.VMEM((HEADS // 2, 2 * keys, 4 * width // HEADS), BF16),
             pltpu.VMEM((points, width), BF16),
-            pltpu.SemaphoreType.DMA((3 + 2 * CHUNKS,)),
-            pltpu.SemaphoreType.DMA((CHUNKS,)),
+            pltpu.SemaphoreType.DMA((CHUNKS * PIECES + 1,)),
         ],
-    )(queries, pairs, bias, grid, w_o_dec, latent_out)
+        compiler_params=pltpu.CompilerParams(vmem_limit_bytes=VMEM_LIMIT),
+    )(latent_out, pairs, queries, bias, grid, w_o_dec)
 
 
 def by_kernels(grid, latent_in, grid_gain, node_gain, dec_gain, w_q_enc, w_kv_enc, w_o_enc,
                w_q_dec, w_kv_dec, w_o_dec, enc_need, enc_slot, enc_count, dec_need, dec_slot):
-    latent_out, pairs, queries, bias = encode(
-        grid, latent_in, grid_gain, node_gain, dec_gain, w_q_enc, w_kv_enc, w_o_enc, w_q_dec, w_kv_dec,
-        enc_need, enc_slot, enc_count, dec_slot, dec_need)
-    grid_out, latent_out = decode(queries, pairs, bias, grid, w_o_dec, latent_out)
-    return (latent_out, grid_out)
+    return decode(*encode(
+        grid, latent_in, grid_gain, node_gain, dec_gain, w_q_enc, w_kv_enc, w_o_enc, w_q_dec, w_kv_dec, w_o_dec,
+        enc_need, enc_slot, enc_count, dec_slot, dec_need))
 
 
 def chosen_form(*args):

time: 38.7 us -> 34.9 us (0.902)
  Pallas kernels: 37.9 us -> 34 us
    pallas_call x1, Pallas kernels: 8.07 us -> 4.95 us  [decode(): pl.pallas_call(decoder_kernel, name='decode', out_shape=(jax.ShapeDtypeSt...]
    pallas_call x1, Pallas kernels: 29.8 us -> 29.1 us  [encode(): pl.pallas_call(functools.partial(encoder_kernel, peers), name='encode', o...]
where the time goes in v2:
time: 34.9 us; the launch traced here: 34.7 us
  Pallas kernels  34 us (97%)
  between operations  0.64 us (2%)
    pallas_call x1, Pallas kernels, encode(): pl.pallas_call(functools.partial(encoder_kernel, peers), name='encode', o...  29.1 us
    pallas_call x1, Pallas kernels, decode(): pl.pallas_call(decoder_kernel, name='decode', out_shape=(jax.ShapeDtypeSt...  4.95 us

profile of v2, /device:TPU:1, one launch (start us, length us, event | category | flops | bytes accessed | tf_op | source)
XLA Modules:
  0.0 34.7 jit_solution(17400366079323079515)
XLA Ops:
  0.6 29.1 %encode.1 = (bf16[16,1024]{1,0:T(8,128)(2,1)S(1)}, bf16[256,1024]{1,0:T(8,128)(2,1)S(1)}, bf16[1024,512]{1,0:T(8,128)(2,1)S(1)}, f32[1024,256]{1,0:T(8,128)S(1)}...) custom-call(bf16[1024,1024]{1,0:T(8,128)(2,1)} %grid_hbm.1, bf16[16,1024]{1,0:T(8,128)(2,1)} %latent_hbm.1, ...), custom_call_target="tpu_custom_call" | custom-call | tf_op jit(solution)/shard_map/encode/pallas_call | solution.py:399
  29.7 4.9 %decode.1 = (bf16[16,1024]{1,0:T(8,128)(2,1)}, bf16[1024,1024]{1,0:T(8,128)(2,1)}) custom-call(bf16[16,1024]{1,0:T(8,128)(2,1)S(1)} %get-tuple-element.8.latent_ref, bf16[256,1024]{1,0:T(8,128)(2,1)S(1)} %get-tuple-element.9.pairs_v, bf16[1024,512]{1,0:T(8,128)(2,1)S(1)} %get-tuple-element.10.query_v, f32[1024,256]{1,0:T(8,128)S(1)} %get-tuple-element.11.bias_v, ...), custom_call_target="tpu_custom_call" | custom-call | tf_op jit(solution)/shard_map/decode/pallas_call | solution.py:499

commit v3 on v2

--- a/solution.py
+++ b/solution.py
@@ -92,9 +92,9 @@
     need_hbm, slot_hbm, count_hbm, dslot_hbm, table_hbm, wod_hbm,
     latent_new, pairs_out, queries_out, bias_out, grid_v, wod_v,
     latent_v, ggain_v, ngain_v, dgain_v, wq_v, wkv_v, wo_v, wqd_v, wkvd_v, need_v, slot_v, count_v, dslot_v,
-    table_v, normed, chosen, rows, fan_of, query_mine, edges_mine,
-    need_all, query_all, edges_all, mix_send, stat_send, mix_all, stat_all, pairs_all,
-    node_of, worth_of, load_sem, send_sem, recv_sem, push_send, push_recv,
+    table_v, normed, band_pairs, rows, query_mine, edges_mine,
+    need_all, query_all, edges_all, latents_all, fresh_all, mix_send, stat_send, mix_all, stat_all, mixes_all, pairs_mine, pairs_in,
+    node_of, worth_of, load_sem, send_sem, recv_sem, push_send, push_recv, pair_send, pair_recv,
 ):
     me = lax.axis_index("dom")
     nodes, model = latent_v.shape
@@ -108,6 +108,9 @@
     points = grid_v.shape[0]
     lanes = HEADS * nodes
     both = 2 * cap
+    quad = 4
+    here = me // 2
+    beside = here + 1 - 2 * lax.rem(here, 2)
     blocks = push_send.shape[0]
     block = points // blocks
 
@@ -147,11 +150,14 @@
     def chip(step):
         return lax.rem(me + 2 * step, peers)
 
+    def place(step):
+        return lax.rem(here + step, chips)
+
     def need_to(step, slot):
         return message(0, need_v, need_all.at[slot], chip(step), step, slot)
 
     def edges_to(step, slot):
-        return message(1, edges_mine.at[chip(step) // group], edges_all.at[slot], chip(step), step, slot)
+        return message(1, edges_mine.at[place(step)], edges_all.at[slot], chip(step), step, slot)
 
     def query_to(step, slot):
         return message(2, query_mine, query_all.at[slot], chip(step), step, slot)
@@ -162,24 +168,40 @@
     def stat_to(step, slot):
         return message(4, stat_send.at[step], stat_all.at[slot], chip(step), step, slot)
 
-    def pairs_to(step, slot):
-        return message(5, pairs_all.at[me], pairs_all.at[me], chip(step), step, slot)
-
-    def pairs_on(step, slot):
-        owner = chip(step)
-        return message(6, pairs_all.at[owner], pairs_all.at[owner], partner, step, slot)
+    def mixes_to(step, slot, owner):
+        return message(5, mixes_all.at[owner], mixes_all.at[owner], chip(step), step, slot)
+
+    def latent_to(step, slot, owner):
+        return message(6, latent_v, latents_all.at[owner], chip(step), step, slot)
+
+    def latent_beside(owner):
+        return message(6, latent_v, latents_all.at[owner], 2 * beside + side, 1, 1)
+
+    def latent_on(step, owner):
+        return message(7, latents_all.at[owner], latents_all.at[owner], 2 * beside + side, step, step)
+
+    def pair_over(number):
+        return pltpu.make_async_remote_copy(
+            src_ref=pairs_mine.at[number],
+            dst_ref=pairs_in.at[number],
+            send_sem=pair_send.at[number],
+            recv_sem=pair_recv.at[number],
+            device_id={"dom": partner},
+            device_id_type=pl.DeviceIdType.MESH,
+        )
 
     def push(number):
         return pltpu.make_async_remote_copy(
-            src_ref=normed.at[0, block_at(number)],
-            dst_ref=normed.at[1, block_at(number)],
+            src_ref=band_pairs.at[0, block_at(number)],
+            dst_ref=band_pairs.at[1, block_at(number)],
             send_sem=push_send.at[number],
             recv_sem=push_recv.at[number],
             device_id={"dom": partner},
             device_id_type=pl.DeviceIdType.MESH,
         )
 
-    others = range(1, chips)
+    others = [step for low in range(1, chips // 2) for step in (low, chips - low)] + [chips // 2]
+    alike = range(2, chips, 2)
 
     loads["slot"].wait()
     loads["count"].wait()
@@ -192,13 +214,10 @@
     for j in range(edge_total):
         tally = tally + jnp.where(slots[:, j : j + 1] == entry, 1.0, 0.0)
     tally = tally.astype(BF16)
-    for part in range(peers // group):
-        edges_mine[part] = tally[:, part * 128 : (part + 1) * 128]
-    edges_all[0] = edges_mine[me // group]
-    fan_row = iota((chips * nodes, chips * lanes), 0)
-    fan_lane = iota((chips * nodes, chips * lanes), 1)
-    fan = fan_row == (fan_lane // lanes) * nodes + lax.rem(fan_lane, nodes)
-    fan_of[...] = jnp.where(fan, 1.0, 0.0).astype(BF16)
+    for number in range(chips):
+        own_part = tally[:, number * both : (number + 1) * both]
+        edges_mine[number] = jnp.concatenate([own_part] * (128 // both), axis=1)
+    edges_all[0] = edges_mine[here]
     loads["need"].wait()
     need_all[0] = need_v[...]
     loads["latent"].wait()
@@ -209,6 +228,7 @@
     ).astype(BF16)
     query_mine[...] = queries
     query_all[0] = queries
+    latents_all[here] = latent_v[...]
 
     pl.semaphore_wait(barrier, chips)
     for step in others:
@@ -220,14 +240,18 @@
     loads["ggain"].wait()
     for number in range(blocks):
         loads[number].wait()
-
-        def norm_block(piece, carry):
-            at = pl.ds(pl.multiple_of(number * block + piece * 128, 128), 128)
-            normed[0, at, :] = norm_into(grid_v[at, :], ggain_v[...])
-            return carry
-
-        lax.fori_loop(0, block // 128, norm_block, 0)
+    loads["wkv"].wait()
+    settled = norm_into(grid_v[block_at(0), :], ggain_v[...])
+    for number in range(blocks):
+        at = block_at(number)
+        normed[at, :] = settled
+        band_pairs[0, at, :] = jnp.dot(settled, wkv_v[...], preferred_element_type=F32).astype(BF16)
+        if number + 1 < blocks:
+            settled = norm_into(grid_v[block_at(number + 1), :], ggain_v[...])
         push(number).start()
+    for step in alike:
+        latent_to(step, chips - step, here).start()
+    latent_beside(here).start()
 
     for step in others:
         need_to(step, step).wait_recv()
@@ -242,59 +266,100 @@
         picked = jnp.where(lane == within + band * cap + spot, asked, 0.0)
         wanted.append(jnp.sum(picked, axis=2, keepdims=True).astype(jnp.int32).reshape(chips * cap, 1))
     point = iota((chips * cap, points), 1)
-    pick = jnp.where(wanted[0] == point, 1.0, 0.0).astype(BF16)
-    chosen[: chips * cap] = jnp.dot(pick, normed[0], preferred_element_type=F32).astype(BF16)
-    pick = jnp.where(wanted[1] == point, 1.0, 0.0).astype(BF16)
+    def rows_of(band):
+        pick = jnp.where(wanted[band] == point, 1.0, 0.0).astype(BF16)
+        return jnp.dot(pick, band_pairs[band], preferred_element_type=F32).astype(BF16)
+
+    rows[side] = rows_of(0)
     for number in range(blocks):
         push(number).wait_recv()
-    chosen[chips * cap :] = jnp.dot(pick, normed[1], preferred_element_type=F32).astype(BF16)
-    loads["wkv"].wait()
-    rows[...] = jnp.dot(chosen[...], wkv_v[...], preferred_element_type=F32).astype(BF16)
+    rows[1 - side] = rows_of(1)
 
     for step in others:
         edges_to(step, step).wait_recv()
-    spot = iota((both, 128), 0)
-    band = jnp.where(spot < cap, side, 1 - side)
-    mine = iota((both, 128), 1) == within + band * cap + lax.rem(spot, cap)
-    entries = lax.dot_general(
-        jnp.where(mine, 1.0, 0.0).astype(BF16), edges_all[...].reshape(chips * nodes, 128), NT,
-        preferred_element_type=F32,
-    ).astype(BF16)
-    entries = jnp.dot(entries, fan_of[...], preferred_element_type=F32)
-    for step in others:
         query_to(step, step).wait_recv()
 
-    own_head = iota((lanes, width), 0) // nodes == iota((lanes, width), 1) // head
-
-    def window(w):
-        spread_query = jnp.broadcast_to(query_all[w][None], (HEADS, nodes, width)).reshape(lanes, width)
-        spread_query = jnp.where(own_head, spread_query, jnp.zeros_like(spread_query))
-        near = slice(w * cap, (w + 1) * cap)
-        far = slice((chips + w) * cap, (chips + w + 1) * cap)
-        keys_here = jnp.concatenate([rows[near, :width], rows[far, :width]], axis=0)
-        values_here = jnp.concatenate([rows[near, width:], rows[far, width:]], axis=0)
-        scores = lax.dot_general(keys_here, spread_query, NT, preferred_element_type=F32)
-        times = entries[:, w * lanes : (w + 1) * lanes]
-        scores = jnp.where(times > 0, scores * (1.0 / math.sqrt(head)), -1e30)
-        highest = jnp.max(scores, axis=0, keepdims=True)
-        raised = jnp.exp(scores - highest) * times
-        total = jnp.sum(raised, axis=0, keepdims=True)
-        mixed = lax.dot_general(raised.astype(BF16), values_here, TN, preferred_element_type=F32)
-        mixed = jnp.where(own_head, mixed, 0.0).reshape(HEADS, nodes, width)
-        return jnp.sum(mixed, axis=0).astype(BF16), highest, total
-
-    for step, answer in [(step, window(step)) for step in range(chips)]:
-        mixes, stats = (mix_all, stat_all) if step == 0 else (mix_send, stat_send)
-        mixes[step] = answer[0]
-        stats[step, 0:1, :] = answer[1]
-        stats[step, 1:2, :] = answer[2]
+    scale = math.log2(math.e) / math.sqrt(head)
+    span = quad * head
+    own_head = iota((quad * nodes, span), 0) // nodes == iota((quad * nodes, span), 1) // head
+    tasks = [(step, four) for step in range(chips) for four in range(HEADS // quad)]
+
+    def score(step, four):
+        lane = slice(four * span, (four + 1) * span)
+        at = slice(step * cap, (step + 1) * cap)
+        query = jnp.concatenate([query_all[step][:, lane]] * quad, axis=0)
+        query = jnp.where(own_head, query, jnp.zeros_like(query))
+        keys_here = jnp.concatenate([rows[0, at, lane], rows[1, at, lane]], axis=0)
+        return lax.dot_general(query, keys_here, NT, preferred_element_type=F32)
+
+    def soften(step, scores):
+        times = jnp.concatenate([edges_all[step][:, :both].astype(F32)] * quad, axis=0)
+        scores = jnp.where(times > 0, scores * scale, -1e30)
+        highest = jnp.max(scores, axis=1, keepdims=True)
+        raised = jnp.exp2(scores - highest) * times
+        return raised.astype(BF16), jnp.broadcast_to(highest, (quad * nodes, 128))
+
+    def blend(step, four, raised):
+        lane = slice(width + four * span, width + (four + 1) * span)
+        at = slice(step * cap, (step + 1) * cap)
+        values_here = jnp.concatenate([rows[0, at, lane], rows[1, at, lane]], axis=0)
+        mixed = jnp.dot(raised, values_here, preferred_element_type=F32)
+        mixed = jnp.where(own_head, mixed, 0.0)
+        return functools.reduce(jnp.add, [mixed[j * nodes : (j + 1) * nodes] for j in range(quad)]).astype(BF16)
+
+    stat_lane = iota((lanes, 128), 1)
+    board = jnp.zeros((lanes, 128), F32)
+    every = jnp.ones((both, 128), BF16)
+    for first in range(0, len(tasks), WAVE):
+        wave = tasks[first : first + WAVE]
+        scored = [score(step, four) for step, four in wave]
+        softened = [soften(step, one) for (step, four), one in zip(wave, scored)]
+        for (step, four), one in zip(wave, softened):
+            mixes = mix_all if step == 0 else mix_send
+            mixes[step, :, four * span : (four + 1) * span] = blend(step, four, one[0])
+        for number in range(0, len(wave), HEADS // quad):
+            step = wave[number][0]
+            group_of = softened[number : number + HEADS // quad]
+            totals = [jnp.dot(one[0], every, preferred_element_type=F32) for one in group_of]
+            board = jnp.where(stat_lane == step, jnp.concatenate([one[1] for one in group_of], axis=0), board)
+            board = jnp.where(stat_lane == chips + step, jnp.concatenate(totals, axis=0), board)
+    board = board.T
+    for step in range(chips):
+        stats = stat_all if step == 0 else stat_send
+        stats[step, 0:1, :] = board[step : step + 1]
+        stats[step, 1:2, :] = board[chips + step : chips + step + 1]
     for step in others:
         mix_to(step, chips - step).start()
         stat_to(step, chips - step).start()
 
+    for step in alike:
+        latent_to(step, step, place(step)).wait_recv()
+        latent_on(step, place(step)).start()
+
     loads["wqd"].wait()
-    scale = math.log2(math.e) / math.sqrt(head)
-    queries_out[...] = (jnp.dot(normed[0], wqd_v[...], preferred_element_type=F32) * scale).astype(BF16)
+    queries_out[...] = (jnp.dot(normed[...], wqd_v[...], preferred_element_type=F32) * scale).astype(BF16)
+
+    loads["wo"].wait()
+    loads["dgain"].wait()
+    loads["wkvd"].wait()
+
+    for step in others:
+        stat_to(step, step).wait_recv()
+    tops = [stat_all[step, 0:1, :] for step in range(chips)]
+    sums = [stat_all[step, 1:2, :] for step in range(chips)]
+    top = functools.reduce(jnp.maximum, tops)
+    shares = [jnp.exp2(one - top) for one in tops]
+    whole = functools.reduce(jnp.add, [a * b for a, b in zip(shares, sums)])
+    own_node = iota((nodes, lanes), 0) == lax.rem(iota((nodes, lanes), 1), nodes)
+    stacked = jnp.concatenate([jnp.where(own_node, share / whole, 0.0) for share in shares], axis=0)
+    widen = (iota((lanes, width), 0) // nodes == iota((lanes, width), 1) // head).astype(F32)
+    factors = jnp.dot(stacked, widen, precision=HIGH, preferred_element_type=F32).reshape(chips, nodes, width)
+    for step in others:
+        mix_to(step, step).wait_recv()
+    enc_mixed = jnp.sum(factors * mix_all[...].astype(F32), axis=0).astype(BF16)
+    mixes_all[here] = enc_mixed
+    for step in others:
+        mixes_to(step, chips - step, here).start()
 
     loads["dslot"].wait()
     loads["table"].wait()
@@ -312,7 +377,8 @@
         for line in range(table_v.shape[0]):
             entry = jnp.broadcast_to(table_v[line : line + 1, :], piece.shape)
             need = jnp.where(high == line, jnp.take_along_axis(entry, low, axis=1), need)
-        columns.append((piece // dec_cap) * nodes + need)
+        owner = piece // dec_cap
+        columns.append(lax.rem(owner, 2) * (chips * nodes) + (owner // 2) * nodes + need)
     node = jnp.concatenate(columns, axis=1)
     times = jnp.ones(node.shape, F32)
     for j in range(1, edge_total):
@@ -331,51 +397,46 @@
         return carry
 
     lax.fori_loop(0, points // 128, bias_block, 0)
-    loads["wo"].wait()
-    loads["dgain"].wait()
-    loads["wkvd"].wait()
-
-    for step in others:
-        stat_to(step, step).wait_recv()
-    tops = [stat_all[step, 0:1, :] for step in range(chips)]
-    sums = [stat_all[step, 1:2, :] for step in range(chips)]
-    top = functools.reduce(jnp.maximum, tops)
-    shares = [jnp.exp(one - top) for one in tops]
-    whole = functools.reduce(jnp.add, [a * b for a, b in zip(shares, sums)])
-    own_node = iota((nodes, lanes), 0) == lax.rem(iota((nodes, lanes), 1), nodes)
-    stacked = jnp.concatenate([jnp.where(own_node, share / whole, 0.0) for share in shares], axis=0)
-    widen = (iota((lanes, width), 0) // nodes == iota((lanes, width), 1) // head).astype(F32)
-    factors = jnp.dot(stacked, widen, precision=HIGH, preferred_element_type=F32).reshape(chips, nodes, width)
-    for step in others:
-        mix_to(step, step).wait_recv()
-    enc_mixed = jnp.sum(factors * mix_all[...].astype(F32), axis=0).astype(BF16)
-    update = jnp.dot(enc_mixed, wo_v[...], preferred_element_type=F32)
-    fresh = (latent_v[...].astype(F32) + update).astype(BF16)
-    latent_new[...] = fresh
-    pairs = jnp.dot(norm_into(fresh, dgain_v[...]), wkvd_v[...], preferred_element_type=F32).astype(BF16)
-    pairs_all[me] = pairs
-    for step in others:
-        pairs_to(step, chips - step).start()
-    pairs_near = message(6, pairs_all.at[me], pairs_all.at[me], partner, 0, 0)
-    pairs_near.start()
-
-    for step in others:
-        pairs_to(step, step).wait_recv()
-        pairs_on(step, step).start()
-    pairs_near.wait_recv()
-    for step in others:
-        pairs_on(step, step).wait_recv()
-    pairs_out[...] = pairs_all[...].reshape(pairs_out.shape)
-
-    for step in others:
-        for outgoing in (need_to, edges_to, query_to, mix_to, stat_to, pairs_to, pairs_on):
+
+    latent_beside(beside).wait_recv()
+    for step in alike:
+        latent_on(step, lax.rem(beside + step, chips)).wait_recv()
+    for step in others:
+        mixes_to(step, step, place(step)).wait_recv()
+    side_nodes = chips * nodes
+    update = jnp.dot(mixes_all[...].reshape(side_nodes, width), wo_v[...], preferred_element_type=F32)
+    fresh = (latents_all[...].reshape(side_nodes, model).astype(F32) + update).astype(BF16)
+    fresh_all[...] = fresh.reshape(chips, nodes, model)
+    settled = norm_into(fresh, dgain_v[...])
+    for number in range(2):
+        half = jnp.dot(settled, wkvd_v[:, number * width : (number + 1) * width], preferred_element_type=F32).astype(BF16)
+        pairs_mine[number] = half
+        pair_over(number).start()
+    latent_new[...] = fresh_all[here]
+    near = pl.ds(pl.multiple_of(side * side_nodes, side_nodes), side_nodes)
+    over = pl.ds(pl.multiple_of((1 - side) * side_nodes, side_nodes), side_nodes)
+    for number in range(2):
+        pairs_out[number, near, :] = pairs_mine[number]
+    for number in range(2):
+        pair_over(number).wait_recv()
+        pairs_out[number, over, :] = pairs_in[number]
+
+    for step in others:
+        for outgoing in (need_to, edges_to, query_to, mix_to, stat_to):
             outgoing(step, step).wait_send()
-    pairs_near.wait_send()
+        mixes_to(step, step, here).wait_send()
+    for step in alike:
+        latent_to(step, step, here).wait_send()
+        latent_on(step, place(step)).wait_send()
+    latent_beside(here).wait_send()
     for number in range(blocks):
         push(number).wait_send()
+    for number in range(2):
+        pair_over(number).wait_send()
     loads["wod"].wait()
 
 
+WAVE = 16
 BLOCKS = 4
 
 
@@ -401,7 +462,7 @@
         name="encode",
         out_shape=(
             pltpu.VMEM((nodes, model), BF16),
-            pltpu.VMEM((peers * nodes, 2 * width), BF16),
+            pltpu.VMEM((2, peers * nodes, width), BF16),
             pltpu.VMEM((points, width), BF16),
             pltpu.VMEM((points, peers * nodes), F32),
             pltpu.VMEM(grid.shape, BF16),
@@ -410,27 +471,32 @@
         in_specs=[far] * len(operands),
         out_specs=(vmem,) * 6,
         scratch_shapes=[pltpu.VMEM(one.shape, one.dtype) for one in operands[1:-1]] + [
-            pltpu.VMEM((2, points, model), BF16),
-            pltpu.VMEM((entries, model), BF16),
-            pltpu.VMEM((entries, 2 * width), BF16),
-            pltpu.VMEM((chips * nodes, chips * lanes), BF16),
+            pltpu.VMEM((points, model), BF16),
+            pltpu.VMEM((2, points, 2 * width), BF16),
+            pltpu.VMEM((2, chips * cap, 2 * width), BF16),
             pltpu.VMEM((nodes, width), BF16),
-            pltpu.VMEM((entries // 128, nodes, 128), BF16),
+            pltpu.VMEM((chips, nodes, 128), BF16),
             pltpu.VMEM((chips, 1, entries), jnp.int32),
             pltpu.VMEM((chips, nodes, width), BF16),
             pltpu.VMEM((chips, nodes, 128), BF16),
+            pltpu.VMEM((chips, nodes, model), BF16),
+            pltpu.VMEM((chips, nodes, model), BF16),
             pltpu.VMEM((chips, nodes, width), BF16),
             pltpu.VMEM((chips, 2, lanes), F32),
             pltpu.VMEM((chips, nodes, width), BF16),
             pltpu.VMEM((chips, 2, lanes), F32),
-            pltpu.VMEM((peers, nodes, 2 * width), BF16),
+            pltpu.VMEM((chips, nodes, width), BF16),
+            pltpu.VMEM((2, chips * nodes, width), BF16),
+            pltpu.VMEM((2, chips * nodes, width), BF16),
             pltpu.VMEM((points, 8), F32),
             pltpu.VMEM((points, 8), F32),
             pltpu.SemaphoreType.DMA((len(operands) - 1 + BLOCKS,)),
-            pltpu.SemaphoreType.DMA((7, chips)),
-            pltpu.SemaphoreType.DMA((7, chips)),
+            pltpu.SemaphoreType.DMA((8, chips)),
+            pltpu.SemaphoreType.DMA((8, chips)),
             pltpu.SemaphoreType.DMA((BLOCKS,)),
             pltpu.SemaphoreType.DMA((BLOCKS,)),
+            pltpu.SemaphoreType.DMA((2,)),
+            pltpu.SemaphoreType.DMA((2,)),
         ],
         compiler_params=pltpu.CompilerParams(collective_id=0, has_side_effects=True, vmem_limit_bytes=VMEM_LIMIT),
     )(*[pltpu.with_memory_space_constraint(one, pltpu.HBM) for one in operands])
@@ -440,7 +506,7 @@
                    out_v, keys_of, values_of, mixed, store_sem):
     points, width = query_v.shape
     head = width // HEADS
-    keys = pairs_v.shape[0]
+    keys = pairs_v.shape[1]
     quad = 4
     chunks = CHUNKS
     tile = points // chunks
@@ -452,11 +518,11 @@
     stores[0].start()
     lane_head = iota((keys, quad * head), 1) // head
     for h in range(HEADS):
-        some = pairs_v[:, (h // quad) * quad * head : (h // quad + 1) * quad * head]
+        some = pairs_v[0, :, (h // quad) * quad * head : (h // quad + 1) * quad * head]
         keys_of[h] = jnp.where(lane_head == h % quad, some, jnp.zeros_like(some))
     side_of = iota((keys, 2 * head), 1) // head
     for pair in range(HEADS // 2):
-        some = pairs_v[:, width + pair * 2 * head : width + (pair + 1) * 2 * head]
+        some = pairs_v[1, :, pair * 2 * head : (pair + 1) * 2 * head]
         for side in range(2):
             own = side_of == side
             at = slice(side * keys, (side + 1) * keys)
@@ -493,7 +559,7 @@
 def decode(latent_out, pairs, queries, bias, grid, w_o_dec):
     points, model = grid.shape
     width = queries.shape[1]
-    keys = pairs.shape[0]
+    keys = pairs.shape[1]
     vmem = pl.BlockSpec(memory_space=pltpu.VMEM)
     far = pl.BlockSpec(memory_space=pltpu.HBM)
     return pl.pallas_call(
@@ -528,7 +594,7 @@
     peers = lax.axis_size("dom")
     cap = enc_need.shape[1] // peers
     small = latent_in.shape[0] * peers <= 256
-    fits = peers % 2 == 0 and 128 % cap == 0 and cap in (32, 64) and HEADS * latent_in.shape[0] == 128 and grid.shape[0] % 512 == 0
+    fits = peers % 4 == 0 and 128 % cap == 0 and cap in (32, 64) and peers <= 128 and HEADS * latent_in.shape[0] == 128 and grid.shape[0] % 512 == 0
     if small and fits and 8 % dec_slot.shape[0] == 0:
         return by_kernels(*args)
     return on_device(*args)

time: 34.9 us -> 31.7 us (0.908)
  Pallas kernels: 34 us -> 30.8 us
    pallas_call x1, Pallas kernels: 29.1 us -> 25.9 us  [encode(): pl.pallas_call(functools.partial(encoder_kernel, peers), name='encode', o...]
where the time goes in v3:
time: 31.7 us; the launch traced here: 31.4 us
  Pallas kernels  30.8 us (97%)
  between operations  0.64 us (2%)
    pallas_call x1, Pallas kernels, encode(): pl.pallas_call(functools.partial(encoder_kernel, peers), name='encode', o...  25.9 us
    pallas_call x1, Pallas kernels, decode(): pl.pallas_call(decoder_kernel, name='decode', out_shape=(jax.ShapeDtypeSt...  4.94 us

profile of v3, /device:TPU:1, one launch (start us, length us, event | category | flops | bytes accessed | tf_op | source)
XLA Modules:
  0.0 31.4 jit_solution(16512571978418759902)
XLA Ops:
  0.6 25.9 %encode.1 = (bf16[16,1024]{1,0:T(8,128)(2,1)S(1)}, bf16[2,256,512]{2,1,0:T(8,128)(2,1)S(1)}, bf16[1024,512]{1,0:T(8,128)(2,1)S(1)}, f32[1024,256]{1,0:T(8,128)S(...) custom-call(bf16[1024,1024]{1,0:T(8,128)(2,1)} %grid_hbm.1, bf16[16,1024]{1,0:T(8,128)(2,1)} %latent_hbm.1, ...), custom_call_target="tpu_custom_call" | custom-call | tf_op jit(solution)/shard_map/encode/pallas_call | solution.py:460
  26.5 4.9 %decode.1 = (bf16[16,1024]{1,0:T(8,128)(2,1)}, bf16[1024,1024]{1,0:T(8,128)(2,1)}) custom-call(bf16[16,1024]{1,0:T(8,128)(2,1)S(1)} %get-tuple-element.8.latent_ref, bf16[2,256,512]{2,1,0:T(8,128)(2,1)S(1)} %get-tuple-element.9.pairs_v, bf16[1024,512]{1,0:T(8,128)(2,1)S(1)} %get-tuple-element.10.query_v, f32[1024,256]{1,0:T(8,128)S(1)} %get-tuple-element.11.bias_v, ...), custom_call_target="tpu_custom_call" | custom-call | tf_op jit(solution)/shard_map/decode/pallas_call | solution.py:565

commit v4 on v3

--- a/solution.py
+++ b/solution.py
@@ -93,8 +93,8 @@
     latent_new, pairs_out, queries_out, bias_out, grid_v, wod_v,
     latent_v, ggain_v, ngain_v, dgain_v, wq_v, wkv_v, wo_v, wqd_v, wkvd_v, need_v, slot_v, count_v, dslot_v,
     table_v, normed, band_pairs, rows, query_mine, edges_mine,
-    need_all, query_all, edges_all, latents_all, fresh_all, mix_send, stat_send, mix_all, stat_all, mixes_all, pairs_mine, pairs_in,
-    node_of, worth_of, load_sem, send_sem, recv_sem, push_send, push_recv, pair_send, pair_recv,
+    need_all, query_all, edges_all, latents_all, mix_send, stat_send, mix_all, stat_all, mixes_all, pairs_mine, pairs_in,
+    node_of, worth_of, load_sem, send_sem, recv_sem, push_sem, pair_send, pair_recv,
 ):
     me = lax.axis_index("dom")
     nodes, model = latent_v.shape
@@ -111,7 +111,7 @@
     quad = 4
     here = me // 2
     beside = here + 1 - 2 * lax.rem(here, 2)
-    blocks = push_send.shape[0]
+    blocks = BLOCKS
     block = points // blocks
 
     barrier = pltpu.get_barrier_semaphore()
@@ -137,12 +137,12 @@
         loads[name] = pltpu.make_async_copy(source, target, load_sem.at[number])
         loads[name].start()
 
-    def message(kind, source, target, to, leaving, landing):
+    def message(kind, source, target, to, landing=None):
         return pltpu.make_async_remote_copy(
             src_ref=source,
             dst_ref=target,
-            send_sem=send_sem.at[kind, leaving],
-            recv_sem=recv_sem.at[kind, landing],
+            send_sem=send_sem.at[kind],
+            recv_sem=recv_sem.at[kind if landing is None else landing],
             device_id={"dom": to},
             device_id_type=pl.DeviceIdType.MESH,
         )
@@ -153,32 +153,53 @@
     def place(step):
         return lax.rem(here + step, chips)
 
-    def need_to(step, slot):
-        return message(0, need_v, need_all.at[slot], chip(step), step, slot)
-
-    def edges_to(step, slot):
-        return message(1, edges_mine.at[place(step)], edges_all.at[slot], chip(step), step, slot)
-
-    def query_to(step, slot):
-        return message(2, query_mine, query_all.at[slot], chip(step), step, slot)
-
-    def mix_to(step, slot):
-        return message(3, mix_send.at[step], mix_all.at[slot], chip(step), step, slot)
-
-    def stat_to(step, slot):
-        return message(4, stat_send.at[step], stat_all.at[slot], chip(step), step, slot)
-
-    def mixes_to(step, slot, owner):
-        return message(5, mixes_all.at[owner], mixes_all.at[owner], chip(step), step, slot)
-
-    def latent_to(step, slot, owner):
-        return message(6, latent_v, latents_all.at[owner], chip(step), step, slot)
-
-    def latent_beside(owner):
-        return message(6, latent_v, latents_all.at[owner], 2 * beside + side, 1, 1)
-
-    def latent_on(step, owner):
-        return message(7, latents_all.at[owner], latents_all.at[owner], 2 * beside + side, step, step)
+    def exchange(kind, buffer):
+        rest = buffer.at[pl.ds(1, chips - 1)]
+        return message(kind, rest, rest, partner)
+
+    def need_to(step):
+        return message(0, need_v, need_all.at[chips - step], chip(step))
+
+    def edges_to(step):
+        return message(1, edges_mine.at[place(step)], edges_all.at[chips - step], chip(step))
+
+    def query_to(step):
+        return message(2, query_mine, query_all.at[chips - step], chip(step))
+
+    def mix_to(step):
+        return message(3, mix_send.at[step], mix_all.at[chips - step], chip(step))
+
+    def stat_to(step):
+        return message(4, stat_send.at[step], stat_all.at[chips - step], chip(step))
+
+    def mixes_to(step):
+        return message(5, mixes_all.at[0], mixes_all.at[chips - step], chip(step))
+
+    apart = chips + here - beside
+
+    def latent_to(step, slot):
+        return message(6, latents_all.at[0], latents_all.at[slot], chip(step), 6 + slot // 2)
+
+    def latent_from(slot):
+        return message(6, latents_all.at[slot], latents_all.at[slot], partner, 6 + slot // 2)
+
+    def latent_on(slot):
+        return message(
+            6, latents_all.at[slot], latents_all.at[lax.rem(slot + apart, chips)], 2 * beside + side, 6
+        )
+
+    def latents_beside():
+        some = latents_all.at[pl.ds(0, chips // 2)]
+        return message(6, some, some, partner, 6)
+
+    push_whole = pltpu.make_async_remote_copy(
+        src_ref=band_pairs.at[0],
+        dst_ref=band_pairs.at[1],
+        send_sem=push_sem.at[0],
+        recv_sem=push_sem.at[1],
+        device_id={"dom": partner},
+        device_id_type=pl.DeviceIdType.MESH,
+    )
 
     def pair_over(number):
         return pltpu.make_async_remote_copy(
@@ -194,8 +215,8 @@
         return pltpu.make_async_remote_copy(
             src_ref=band_pairs.at[0, block_at(number)],
             dst_ref=band_pairs.at[1, block_at(number)],
-            send_sem=push_send.at[number],
-            recv_sem=push_recv.at[number],
+            send_sem=push_sem.at[0],
+            recv_sem=push_sem.at[1],
             device_id={"dom": partner},
             device_id_type=pl.DeviceIdType.MESH,
         )
@@ -228,14 +249,14 @@
     ).astype(BF16)
     query_mine[...] = queries
     query_all[0] = queries
-    latents_all[here] = latent_v[...]
+    latents_all[0] = latent_v[...]
 
     pl.semaphore_wait(barrier, chips)
     for step in others:
-        need_to(step, chips - step).start()
+        need_to(step).start()
     for step in others:
-        edges_to(step, chips - step).start()
-        query_to(step, chips - step).start()
+        edges_to(step).start()
+        query_to(step).start()
 
     loads["ggain"].wait()
     for number in range(blocks):
@@ -250,11 +271,10 @@
             settled = norm_into(grid_v[block_at(number + 1), :], ggain_v[...])
         push(number).start()
     for step in alike:
-        latent_to(step, chips - step, here).start()
-    latent_beside(here).start()
-
-    for step in others:
-        need_to(step, step).wait_recv()
+        latent_to(step, chips - step).start()
+    latent_on(0).start()
+
+    exchange(0, need_all).wait_recv()
     base = pl.multiple_of((me // group) * 128, 128)
     lists = need_all[:, :, pl.ds(base, 128)]
     within = lax.rem(me // 2, group // 2) * both
@@ -266,18 +286,19 @@
         picked = jnp.where(lane == within + band * cap + spot, asked, 0.0)
         wanted.append(jnp.sum(picked, axis=2, keepdims=True).astype(jnp.int32).reshape(chips * cap, 1))
     point = iota((chips * cap, points), 1)
-    def rows_of(band):
-        pick = jnp.where(wanted[band] == point, 1.0, 0.0).astype(BF16)
-        return jnp.dot(pick, band_pairs[band], preferred_element_type=F32).astype(BF16)
-
-    rows[side] = rows_of(0)
-    for number in range(blocks):
-        push(number).wait_recv()
-    rows[1 - side] = rows_of(1)
-
-    for step in others:
-        edges_to(step, step).wait_recv()
-        query_to(step, step).wait_recv()
+    def pick_of(band):
+        return jnp.where(wanted[band] == point, 1.0, 0.0).astype(BF16)
+
+    def rows_of(band, part):
+        lane = slice(part * width, (part + 1) * width)
+        return jnp.dot(pick_of(band), band_pairs[band, :, lane], preferred_element_type=F32).astype(BF16)
+
+    for part in range(2):
+        rows[part, side] = rows_of(0, part)
+    exchange(1, edges_all).wait_recv()
+    exchange(2, query_all).wait_recv()
+    push_whole.wait_recv()
+    rows[0, 1 - side] = rows_of(1, 0)
 
     scale = math.log2(math.e) / math.sqrt(head)
     span = quad * head
@@ -289,7 +310,7 @@
         at = slice(step * cap, (step + 1) * cap)
         query = jnp.concatenate([query_all[step][:, lane]] * quad, axis=0)
         query = jnp.where(own_head, query, jnp.zeros_like(query))
-        keys_here = jnp.concatenate([rows[0, at, lane], rows[1, at, lane]], axis=0)
+        keys_here = jnp.concatenate([rows[0, 0, at, lane], rows[0, 1, at, lane]], axis=0)
         return lax.dot_general(query, keys_here, NT, preferred_element_type=F32)
 
     def soften(step, scores):
@@ -300,9 +321,9 @@
         return raised.astype(BF16), jnp.broadcast_to(highest, (quad * nodes, 128))
 
     def blend(step, four, raised):
-        lane = slice(width + four * span, width + (four + 1) * span)
+        lane = slice(four * span, (four + 1) * span)
         at = slice(step * cap, (step + 1) * cap)
-        values_here = jnp.concatenate([rows[0, at, lane], rows[1, at, lane]], axis=0)
+        values_here = jnp.concatenate([rows[1, 0, at, lane], rows[1, 1, at, lane]], axis=0)
         mixed = jnp.dot(raised, values_here, preferred_element_type=F32)
         mixed = jnp.where(own_head, mixed, 0.0)
         return functools.reduce(jnp.add, [mixed[j * nodes : (j + 1) * nodes] for j in range(quad)]).astype(BF16)
@@ -310,31 +331,29 @@
     stat_lane = iota((lanes, 128), 1)
     board = jnp.zeros((lanes, 128), F32)
     every = jnp.ones((both, 128), BF16)
-    for first in range(0, len(tasks), WAVE):
-        wave = tasks[first : first + WAVE]
-        scored = [score(step, four) for step, four in wave]
-        softened = [soften(step, one) for (step, four), one in zip(wave, scored)]
-        for (step, four), one in zip(wave, softened):
-            mixes = mix_all if step == 0 else mix_send
-            mixes[step, :, four * span : (four + 1) * span] = blend(step, four, one[0])
-        for number in range(0, len(wave), HEADS // quad):
-            step = wave[number][0]
-            group_of = softened[number : number + HEADS // quad]
-            totals = [jnp.dot(one[0], every, preferred_element_type=F32) for one in group_of]
-            board = jnp.where(stat_lane == step, jnp.concatenate([one[1] for one in group_of], axis=0), board)
-            board = jnp.where(stat_lane == chips + step, jnp.concatenate(totals, axis=0), board)
+    scored = [score(step, four) for step, four in tasks]
+    rows[1, 1 - side] = rows_of(1, 1)
+    softened = [soften(step, one) for (step, four), one in zip(tasks, scored)]
+    for (step, four), one in zip(tasks, softened):
+        mixes = mix_all if step == 0 else mix_send
+        mixes[step, :, four * span : (four + 1) * span] = blend(step, four, one[0])
+    for step in range(chips):
+        pair = softened[step * (HEADS // quad) : (step + 1) * (HEADS // quad)]
+        totals = [jnp.dot(one[0], every, preferred_element_type=F32) for one in pair]
+        board = jnp.where(stat_lane == step, jnp.concatenate([one[1] for one in pair], axis=0), board)
+        board = jnp.where(stat_lane == chips + step, jnp.concatenate(totals, axis=0), board)
     board = board.T
     for step in range(chips):
         stats = stat_all if step == 0 else stat_send
         stats[step, 0:1, :] = board[step : step + 1]
         stats[step, 1:2, :] = board[chips + step : chips + step + 1]
     for step in others:
-        mix_to(step, chips - step).start()
-        stat_to(step, chips - step).start()
+        mix_to(step).start()
+        stat_to(step).start()
 
     for step in alike:
-        latent_to(step, step, place(step)).wait_recv()
-        latent_on(step, place(step)).start()
+        latent_from(step).wait_recv()
+        latent_on(step).start()
 
     loads["wqd"].wait()
     queries_out[...] = (jnp.dot(normed[...], wqd_v[...], preferred_element_type=F32) * scale).astype(BF16)
@@ -343,8 +362,7 @@
     loads["dgain"].wait()
     loads["wkvd"].wait()
 
-    for step in others:
-        stat_to(step, step).wait_recv()
+    exchange(4, stat_all).wait_recv()
     tops = [stat_all[step, 0:1, :] for step in range(chips)]
     sums = [stat_all[step, 1:2, :] for step in range(chips)]
     top = functools.reduce(jnp.maximum, tops)
@@ -354,12 +372,11 @@
     stacked = jnp.concatenate([jnp.where(own_node, share / whole, 0.0) for share in shares], axis=0)
     widen = (iota((lanes, width), 0) // nodes == iota((lanes, width), 1) // head).astype(F32)
     factors = jnp.dot(stacked, widen, precision=HIGH, preferred_element_type=F32).reshape(chips, nodes, width)
+    exchange(3, mix_all).wait_recv()
+    enc_mixed = jnp.sum(factors * mix_all[...].astype(F32), axis=0).astype(BF16)
+    mixes_all[0] = enc_mixed
     for step in others:
-        mix_to(step, step).wait_recv()
-    enc_mixed = jnp.sum(factors * mix_all[...].astype(F32), axis=0).astype(BF16)
-    mixes_all[here] = enc_mixed
-    for step in others:
-        mixes_to(step, chips - step, here).start()
+        mixes_to(step).start()
 
     loads["dslot"].wait()
     loads["table"].wait()
@@ -378,7 +395,7 @@
             entry = jnp.broadcast_to(table_v[line : line + 1, :], piece.shape)
             need = jnp.where(high == line, jnp.take_along_axis(entry, low, axis=1), need)
         owner = piece // dec_cap
-        columns.append(lax.rem(owner, 2) * (chips * nodes) + (owner // 2) * nodes + need)
+        columns.append(lax.rem(owner, 2) * (chips * nodes) + lax.rem(owner // 2 - here + chips, chips) * nodes + need)
     node = jnp.concatenate(columns, axis=1)
     times = jnp.ones(node.shape, F32)
     for j in range(1, edge_total):
@@ -398,21 +415,17 @@
 
     lax.fori_loop(0, points // 128, bias_block, 0)
 
-    latent_beside(beside).wait_recv()
-    for step in alike:
-        latent_on(step, lax.rem(beside + step, chips)).wait_recv()
-    for step in others:
-        mixes_to(step, step, place(step)).wait_recv()
+    latents_beside().wait_recv()
+    exchange(5, mixes_all).wait_recv()
     side_nodes = chips * nodes
     update = jnp.dot(mixes_all[...].reshape(side_nodes, width), wo_v[...], preferred_element_type=F32)
     fresh = (latents_all[...].reshape(side_nodes, model).astype(F32) + update).astype(BF16)
-    fresh_all[...] = fresh.reshape(chips, nodes, model)
     settled = norm_into(fresh, dgain_v[...])
     for number in range(2):
         half = jnp.dot(settled, wkvd_v[:, number * width : (number + 1) * width], preferred_element_type=F32).astype(BF16)
         pairs_mine[number] = half
         pair_over(number).start()
-    latent_new[...] = fresh_all[here]
+    latent_new[...] = fresh[:nodes]
     near = pl.ds(pl.multiple_of(side * side_nodes, side_nodes), side_nodes)
     over = pl.ds(pl.multiple_of((1 - side) * side_nodes, side_nodes), side_nodes)
     for number in range(2):
@@ -421,22 +434,14 @@
         pair_over(number).wait_recv()
         pairs_out[number, over, :] = pairs_in[number]
 
-    for step in others:
-        for outgoing in (need_to, edges_to, query_to, mix_to, stat_to):
-            outgoing(step, step).wait_send()
-        mixes_to(step, step, here).wait_send()
-    for step in alike:
-        latent_to(step, step, here).wait_send()
-        latent_on(step, place(step)).wait_send()
-    latent_beside(here).wait_send()
-    for number in range(blocks):
-        push(number).wait_send()
+    for kind, buffer in enumerate((need_all, edges_all, query_all, mix_all, stat_all, mixes_all, latents_all)):
+        exchange(kind, buffer).wait_send()
+    push_whole.wait_send()
     for number in range(2):
         pair_over(number).wait_send()
     loads["wod"].wait()
 
 
-WAVE = 16
 BLOCKS = 4
 
 
@@ -473,13 +478,12 @@
         scratch_shapes=[pltpu.VMEM(one.shape, one.dtype) for one in operands[1:-1]] + [
             pltpu.VMEM((points, model), BF16),
             pltpu.VMEM((2, points, 2 * width), BF16),
-            pltpu.VMEM((2, chips * cap, 2 * width), BF16),
+            pltpu.VMEM((2, 2, chips * cap, width), BF16),
             pltpu.VMEM((nodes, width), BF16),
             pltpu.VMEM((chips, nodes, 128), BF16),
             pltpu.VMEM((chips, 1, entries), jnp.int32),
             pltpu.VMEM((chips, nodes, width), BF16),
             pltpu.VMEM((chips, nodes, 128), BF16),
-            pltpu.VMEM((chips, nodes, model), BF16),
             pltpu.VMEM((chips, nodes, model), BF16),
             pltpu.VMEM((chips, nodes, width), BF16),
             pltpu.VMEM((chips, 2, lanes), F32),
@@ -491,10 +495,9 @@
             pltpu.VMEM((points, 8), F32),
             pltpu.VMEM((points, 8), F32),
             pltpu.SemaphoreType.DMA((len(operands) - 1 + BLOCKS,)),
-            pltpu.SemaphoreType.DMA((8, chips)),
-            pltpu.SemaphoreType.DMA((8, chips)),
-            pltpu.SemaphoreType.DMA((BLOCKS,)),
-            pltpu.SemaphoreType.DMA((BLOCKS,)),
+            pltpu.SemaphoreType.DMA((7,)),
+            pltpu.SemaphoreType.DMA((6 + chips // 2,)),
+            pltpu.SemaphoreType.DMA((2,)),
             pltpu.SemaphoreType.DMA((2,)),
             pltpu.SemaphoreType.DMA((2,)),
         ],
@@ -503,7 +506,7 @@
 
 
 def decoder_kernel(latent_ref, pairs_v, query_v, bias_v, grid_v, wo_v, latent_hbm, out_hbm,
-                   out_v, keys_of, values_of, mixed, store_sem):
+                   out_v, mixed, store_sem):
     points, width = query_v.shape
     head = width // HEADS
     keys = pairs_v.shape[1]
@@ -517,17 +520,19 @@
     stores = [pltpu.make_async_copy(latent_ref, latent_hbm, store_sem.at[chunks * PIECES])]
     stores[0].start()
     lane_head = iota((keys, quad * head), 1) // head
-    for h in range(HEADS):
+    side_of = iota((keys, 2 * head), 1) // head
+
+    def keys_of(h):
         some = pairs_v[0, :, (h // quad) * quad * head : (h // quad + 1) * quad * head]
-        keys_of[h] = jnp.where(lane_head == h % quad, some, jnp.zeros_like(some))
-    side_of = iota((keys, 2 * head), 1) // head
-    for pair in range(HEADS // 2):
+        return jnp.where(lane_head == h % quad, some, jnp.zeros_like(some))
+
+    def values_of(pair):
         some = pairs_v[1, :, pair * 2 * head : (pair + 1) * 2 * head]
-        for side in range(2):
-            own = side_of == side
-            at = slice(side * keys, (side + 1) * keys)
-            values_of[pair, at, : 2 * head] = jnp.where(own, some, jnp.zeros_like(some))
-            values_of[pair, at, 2 * head :] = jnp.where(own, jnp.ones_like(some), jnp.zeros_like(some))
+        none, one = jnp.zeros_like(some), jnp.ones_like(some)
+        return jnp.concatenate([
+            jnp.concatenate([jnp.where(side_of == side, some, none), jnp.where(side_of == side, one, none)], axis=1)
+            for side in range(2)
+        ], axis=0)
 
     for part in range(chunks):
         at = rows(part)
@@ -536,11 +541,11 @@
             query = query_v[at, four * quad * head : (four + 1) * quad * head]
             raised = []
             for side in range(2):
-                scores = lax.dot_general(query, keys_of[2 * pair + side], NT, preferred_element_type=F32)
+                scores = lax.dot_general(query, keys_of(2 * pair + side), NT, preferred_element_type=F32)
                 scores = scores + bias_v[at, :]
                 highest = jnp.max(scores, axis=1, keepdims=True)
                 raised.append(jnp.exp2(scores - highest).astype(BF16))
-            got = jnp.dot(jnp.concatenate(raised, axis=1), values_of[pair], preferred_element_type=F32)
+            got = jnp.dot(jnp.concatenate(raised, axis=1), values_of(pair), preferred_element_type=F32)
             mixed[at, pair * 2 * head : (pair + 1) * 2 * head] = (got[:, : 2 * head] / got[:, 2 * head :]).astype(BF16)
         for piece in range(PIECES):
             at = slice(part * tile + piece * (tile // PIECES), part * tile + (piece + 1) * (tile // PIECES))
@@ -552,14 +557,13 @@
         store.wait()
 
 
-CHUNKS = 2
-PIECES = 2
+CHUNKS = 1
+PIECES = 4
 
 
 def decode(latent_out, pairs, queries, bias, grid, w_o_dec):
     points, model = grid.shape
     width = queries.shape[1]
-    keys = pairs.shape[1]
     vmem = pl.BlockSpec(memory_space=pltpu.VMEM)
     far = pl.BlockSpec(memory_space=pltpu.HBM)
     return pl.pallas_call(
@@ -573,8 +577,6 @@
         out_specs=(far, far),
         scratch_shapes=[
             pltpu.VMEM(grid.shape, BF16),
-            pltpu.VMEM((HEADS, keys, width // 2), BF16),
-            pltpu.VMEM((HEADS // 2, 2 * keys, 4 * width // HEADS), BF16),
             pltpu.VMEM((points, width), BF16),
             pltpu.SemaphoreType.DMA((CHUNKS * PIECES + 1,)),
         ],

time: 31.7 us -> 30.1 us (0.950)
  Pallas kernels: 30.8 us -> 29.1 us
    pallas_call x1, Pallas kernels: 25.9 us -> 24.3 us  [encode(): pl.pallas_call(functools.partial(encoder_kernel, peers), name='encode', o...]
where the time goes in v4:
time: 30.1 us; the launch traced here: 29.7 us
  Pallas kernels  29.1 us (97%)
  between operations  0.64 us (2%)
    pallas_call x1, Pallas kernels, encode(): pl.pallas_call(functools.partial(encoder_kernel, peers), name='encode', o...  24.3 us
    pallas_call x1, Pallas kernels, decode(): pl.pallas_call(decoder_kernel, name='decode', out_shape=(jax.ShapeDtypeSt...  4.78 us

profile of v4, /device:TPU:1, one launch (start us, length us, event | category | flops | bytes accessed | tf_op | source)
XLA Modules:
  0.0 29.7 jit_solution(14804743569520628492)
XLA Ops:
  0.6 24.3 %encode.1 = (bf16[16,1024]{1,0:T(8,128)(2,1)S(1)}, bf16[2,256,512]{2,1,0:T(8,128)(2,1)S(1)}, bf16[1024,512]{1,0:T(8,128)(2,1)S(1)}, f32[1024,256]{1,0:T(8,128)S(...) custom-call(bf16[1024,1024]{1,0:T(8,128)(2,1)} %grid_hbm.1, bf16[16,1024]{1,0:T(8,128)(2,1)} %latent_hbm.1, ...), custom_call_target="tpu_custom_call" | custom-call | tf_op jit(solution)/shard_map/encode/pallas_call | solution.py:465
  25.0 4.8 %decode.1 = (bf16[16,1024]{1,0:T(8,128)(2,1)}, bf16[1024,1024]{1,0:T(8,128)(2,1)}) custom-call(bf16[16,1024]{1,0:T(8,128)(2,1)S(1)} %get-tuple-element.8.latent_ref, bf16[2,256,512]{2,1,0:T(8,128)(2,1)S(1)} %get-tuple-element.9.pairs_v, bf16[1024,512]{1,0:T(8,128)(2,1)S(1)} %get-tuple-element.10.query_v, f32[1024,256]{1,0:T(8,128)S(1)} %get-tuple-element.11.bias_v, ...), custom_call_target="tpu_custom_call" | custom-call | tf_op jit(solution)/shard_map/decode/pallas_call | solution.py:569

commit v5 on v4

--- a/solution.py
+++ b/solution.py
@@ -511,13 +511,11 @@
     head = width // HEADS
     keys = pairs_v.shape[1]
     quad = 4
-    chunks = CHUNKS
-    tile = points // chunks
-
-    def rows(part):
-        return slice(part * tile, (part + 1) * tile)
-
-    stores = [pltpu.make_async_copy(latent_ref, latent_hbm, store_sem.at[chunks * PIECES])]
+
+    def rows(part, size):
+        return slice(part * size, (part + 1) * size)
+
+    stores = [pltpu.make_async_copy(latent_ref, latent_hbm, store_sem.at[PIECES])]
     stores[0].start()
     lane_head = iota((keys, quad * head), 1) // head
     side_of = iota((keys, 2 * head), 1) // head
@@ -534,31 +532,39 @@
             for side in range(2)
         ], axis=0)
 
-    for part in range(chunks):
-        at = rows(part)
-        for pair in range(HEADS // 2):
-            four = 2 * pair // quad
-            query = query_v[at, four * quad * head : (four + 1) * quad * head]
-            raised = []
-            for side in range(2):
-                scores = lax.dot_general(query, keys_of(2 * pair + side), NT, preferred_element_type=F32)
-                scores = scores + bias_v[at, :]
-                highest = jnp.max(scores, axis=1, keepdims=True)
-                raised.append(jnp.exp2(scores - highest).astype(BF16))
-            got = jnp.dot(jnp.concatenate(raised, axis=1), values_of(pair), preferred_element_type=F32)
-            mixed[at, pair * 2 * head : (pair + 1) * 2 * head] = (got[:, : 2 * head] / got[:, 2 * head :]).astype(BF16)
-        for piece in range(PIECES):
-            at = slice(part * tile + piece * (tile // PIECES), part * tile + (piece + 1) * (tile // PIECES))
-            update = jnp.dot(mixed[at, :], wo_v[...], preferred_element_type=F32)
-            out_v[at, :] = (grid_v[at, :].astype(F32) + update).astype(BF16)
-            stores.append(pltpu.make_async_copy(out_v.at[at], out_hbm.at[at], store_sem.at[part * PIECES + piece]))
-            stores[-1].start()
+    def attend(pair, at):
+        four = 2 * pair // quad
+        query = query_v[at, four * quad * head : (four + 1) * quad * head]
+        raised = []
+        for side in range(2):
+            scores = lax.dot_general(query, keys_of(2 * pair + side), NT, preferred_element_type=F32)
+            scores = scores + bias_v[at, :]
+            highest = jnp.max(scores, axis=1, keepdims=True)
+            raised.append(jnp.exp2(scores - highest).astype(BF16))
+        got = jnp.dot(jnp.concatenate(raised, axis=1), values_of(pair), preferred_element_type=F32)
+        mixed[at, pair * 2 * head : (pair + 1) * 2 * head] = (got[:, : 2 * head] / got[:, 2 * head :]).astype(BF16)
+
+    def project(number, size):
+        at = slice(number * size, (number + 1) * size)
+        update = jnp.dot(mixed[at, :], wo_v[...], preferred_element_type=F32)
+        out_v[at, :] = (grid_v[at, :].astype(F32) + update).astype(BF16)
+
+    def leave(number, size):
+        at = slice(number * size, (number + 1) * size)
+        stores.append(pltpu.make_async_copy(out_v.at[at], out_hbm.at[at], store_sem.at[number]))
+        stores[-1].start()
+
+    for pair in range(HEADS // 2):
+        for part in range(2):
+            attend(pair, rows(part, points // 2))
+    for number in range(PIECES):
+        project(number, points // PIECES)
+        leave(number, points // PIECES)
     for store in stores:
         store.wait()
 
 
-CHUNKS = 1
-PIECES = 4
+PIECES = 8
 
 
 def decode(latent_out, pairs, queries, bias, grid, w_o_dec):
@@ -578,7 +584,7 @@
         scratch_shapes=[
             pltpu.VMEM(grid.shape, BF16),
             pltpu.VMEM((points, width), BF16),
-            pltpu.SemaphoreType.DMA((CHUNKS * PIECES + 1,)),
+            pltpu.SemaphoreType.DMA((PIECES + 1,)),
         ],
         compiler_params=pltpu.CompilerParams(vmem_limit_bytes=VMEM_LIMIT),
     )(latent_out, pairs, queries, bias, grid, w_o_dec)

time: 30.1 us -> 29.6 us (0.983)
  Pallas kernels: 29.1 us -> 28.7 us
    pallas_call x1, Pallas kernels: 4.78 us -> 4.37 us  [decode(): pl.pallas_call(decoder_kernel, name='decode', out_shape=(jax.ShapeDtypeSt...]
where the time goes in v5:
time: 29.6 us; the launch traced here: 29.3 us
  Pallas kernels  28.7 us (97%)
  between operations  0.64 us (2%)
    pallas_call x1, Pallas kernels, encode(): pl.pallas_call(functools.partial(encoder_kernel, peers), name='encode', o...  24.3 us
    pallas_call x1, Pallas kernels, decode(): pl.pallas_call(decoder_kernel, name='decode', out_shape=(jax.ShapeDtypeSt...  4.37 us

profile of v5, /device:TPU:1, one launch (start us, length us, event | category | flops | bytes accessed | tf_op | source)
XLA Modules:
  0.0 29.3 jit_solution(10427659232612093762)
XLA Ops:
  0.6 24.3 %encode.1 = (bf16[16,1024]{1,0:T(8,128)(2,1)S(1)}, bf16[2,256,512]{2,1,0:T(8,128)(2,1)S(1)}, bf16[1024,512]{1,0:T(8,128)(2,1)S(1)}, f32[1024,256]{1,0:T(8,128)S(...) custom-call(bf16[1024,1024]{1,0:T(8,128)(2,1)} %grid_hbm.1, bf16[16,1024]{1,0:T(8,128)(2,1)} %latent_hbm.1, ...), custom_call_target="tpu_custom_call" | custom-call | tf_op jit(solution)/shard_map/encode/pallas_call | solution.py:465
  25.0 4.4 %decode.1 = (bf16[16,1024]{1,0:T(8,128)(2,1)}, bf16[1024,1024]{1,0:T(8,128)(2,1)}) custom-call(bf16[16,1024]{1,0:T(8,128)(2,1)S(1)} %get-tuple-element.8.latent_ref, bf16[2,256,512]{2,1,0:T(8,128)(2,1)S(1)} %get-tuple-element.9.pairs_v, bf16[1024,512]{1,0:T(8,128)(2,1)S(1)} %get-tuple-element.10.query_v, f32[1024,256]{1,0:T(8,128)S(1)} %get-tuple-element.11.bias_v, ...), custom_call_target="tpu_custom_call" | custom-call | tf_op jit(solution)/shard_map/decode/pallas_call | solution.py:575

commit v6 on v5

--- a/solution.py
+++ b/solution.py
@@ -348,8 +348,8 @@
         stats[step, 0:1, :] = board[step : step + 1]
         stats[step, 1:2, :] = board[chips + step : chips + step + 1]
     for step in others:
+        stat_to(step).start()
         mix_to(step).start()
-        stat_to(step).start()
 
     for step in alike:
         latent_from(step).wait_recv()
@@ -430,16 +430,16 @@
     over = pl.ds(pl.multiple_of((1 - side) * side_nodes, side_nodes), side_nodes)
     for number in range(2):
         pairs_out[number, near, :] = pairs_mine[number]
+    for kind, buffer in enumerate((need_all, edges_all, query_all, mix_all, stat_all, mixes_all, latents_all)):
+        exchange(kind, buffer).wait_send()
+    push_whole.wait_send()
+    loads["wod"].wait()
     for number in range(2):
         pair_over(number).wait_recv()
         pairs_out[number, over, :] = pairs_in[number]
 
-    for kind, buffer in enumerate((need_all, edges_all, query_all, mix_all, stat_all, mixes_all, latents_all)):
-        exchange(kind, buffer).wait_send()
-    push_whole.wait_send()
     for number in range(2):
         pair_over(number).wait_send()
-    loads["wod"].wait()
 
 
 BLOCKS = 4

time: 29.6 us -> 29.6 us (level)
  no operation moved by 1% of the time
where the time goes in v6:
time: 29.6 us; the launch traced here: 29.2 us
  Pallas kernels  28.6 us (97%)
  between operations  0.64 us (2%)
    pallas_call x1, Pallas kernels, encode(): pl.pallas_call(functools.partial(encoder_kernel, peers), name='encode', o...  24.2 us
    pallas_call x1, Pallas kernels, decode(): pl.pallas_call(decoder_kernel, name='decode', out_shape=(jax.ShapeDtypeSt...  4.36 us

profile of v6, /device:TPU:1, one launch (start us, length us, event | category | flops | bytes accessed | tf_op | source)
XLA Modules:
  0.0 29.2 jit_solution(12235970980116348077)
XLA Ops:
  0.6 24.2 %encode.1 = (bf16[16,1024]{1,0:T(8,128)(2,1)S(1)}, bf16[2,256,512]{2,1,0:T(8,128)(2,1)S(1)}, bf16[1024,512]{1,0:T(8,128)(2,1)S(1)}, f32[1024,256]{1,0:T(8,128)S(...) custom-call(bf16[1024,1024]{1,0:T(8,128)(2,1)} %grid_hbm.1, bf16[16,1024]{1,0:T(8,128)(2,1)} %latent_hbm.1, ...), custom_call_target="tpu_custom_call" | custom-call | tf_op jit(solution)/shard_map/encode/pallas_call | solution.py:465
  24.9 4.4 %decode.1 = (bf16[16,1024]{1,0:T(8,128)(2,1)}, bf16[1024,1024]{1,0:T(8,128)(2,1)}) custom-call(bf16[16,1024]{1,0:T(8,128)(2,1)S(1)} %get-tuple-element.8.latent_ref, bf16[2,256,512]{2,1,0:T(8,128)(2,1)S(1)} %get-tuple-element.9.pairs_v, bf16[1024,512]{1,0:T(8,128)(2,1)S(1)} %get-tuple-element.10.query_v, f32[1024,256]{1,0:T(8,128)S(1)} %get-tuple-element.11.bias_v, ...), custom_call_target="tpu_custom_call" | custom-call | tf_op jit(solution)/shard_map/decode/pallas_call | solution.py:575
